TPU v7x, 32 devices: a whole 2x2x4 slice. The times are simulated.
32 devices in a mesh: row: 4 (over z), col: 4 (over x, core), grid: 2 (over y).
Axes of the slice: x: 2, y: 2, z: 4, core: 2. Of those that a mesh axis runs over, the one named last changes fastest.
Arguments:
- tokens: bfloat16 [2, 4096, 2048], P(None, ('row', 'col'), 'grid'), may hold values from -6 to 6
- cotangent: bfloat16 [2, 4096, 2048], P(None, ('row', 'col'), 'grid'), may hold values from -6 to 6
- lengths: int32 [2, 4, 2, 4], replicated, may hold values from 0 to 512, as said below
- deal_pages: int32 [2, 4, 4, 4], replicated, may hold values from 0 to 3, each once within a row
- land_slots: int32 [2, 4, 4, 4], replicated, may hold values from 0 to 3, each once within a row
- pre_gain: float32 [2048], P('grid'), may hold values from 0.5 to 1.5
- pre_bias: float32 [2048], P('grid'), may hold values from -2.5 to 2.5
- query_weight: bfloat16 [2048, 2048], P('grid', 'col'), may hold values from -0.088388348 to 0.088388348
- key_weight: bfloat16 [2048, 2048], P('grid', 'col'), may hold values from -0.088388348 to 0.088388348
- value_weight: bfloat16 [2048, 4096], P('grid', 'col'), may hold values from -0.125 to 0.125
- gate_weight: bfloat16 [2048, 4096], P('grid', 'col'), may hold values from -0.125 to 0.125
- group_gain: float32 [4096], P('col'), may hold values from 0.5 to 1.5
- group_bias: float32 [4096], P('col'), may hold values from -2.5 to 2.5
- output_weight: bfloat16 [4096, 2048], P('col', 'grid'), may hold values from -0.125 to 0.125
- mid_gain: float32 [2048], P('grid'), may hold values from 0.5 to 1.5
- mid_bias: float32 [2048], P('grid'), may hold values from -2.5 to 2.5
- up_weight: bfloat16 [2048, 4096], P('grid', 'col'), may hold values from -0.125 to 0.125
- down_weight: bfloat16 [4096, 2048], P('col', 'grid'), may hold values from -0.125 to 0.125
Outputs:
- block_out: bfloat16 [2, 4096, 2048], P(None, ('row', 'col'), 'grid')
- tokens_grad: bfloat16 [2, 4096, 2048], P(None, ('row', 'col'), 'grid')
- pregain_grad: float32 [2048], P('grid')
- prebias_grad: float32 [2048], P('grid')
- query_grad: float32 [2048, 2048], P('grid', 'col')
- key_grad: float32 [2048, 2048], P('grid', 'col')
- value_grad: float32 [2048, 4096], P('grid', 'col')
- gating_grad: float32 [2048, 4096], P('grid', 'col')
- groupgain_grad: float32 [4096], P('col')
- groupbias_grad: float32 [4096], P('col')
- output_grad: float32 [4096, 2048], P('col', 'grid')
- midgain_grad: float32 [2048], P('grid')
- midbias_grad: float32 [2048], P('grid')
- upward_grad: float32 [2048, 4096], P('grid', 'col')
- downward_grad: float32 [4096, 2048], P('col', 'grid')
Inputs may be any that keep to these rules, and one draw needn't show every extreme that they name: The 4 lengths of a cell sum to 512; a length may be 0; in every micro-batch the cell of row 0 and grid index 0 holds one sequence of 512 tokens. For every micro-batch, column and source row, deal_pages is a permutation of the pages. For every micro-batch, column and destination row, land_slots is a permutation of the slots.
All inputs are finite; a program needn't handle non-finite values.
Results may differ from a plain program's by a relative error of at most 0.018.
Values may be sent and summed in bfloat16 or wider, within the bound.
No kernel may reach another device: no remote copies, remote signals or barrier semaphores. Data moves between devices by JAX's collectives and lax.ppermute only.
A program may use at most 256 MiB of HBM per device.

v0:
```python
import jax
import jax.numpy as jnp
from jax import lax
from jax.sharding import PartitionSpec as P

D = 2048
QK_HEAD = 256
V_HEAD = 512
CH = 512


epsilon = 1e-05


def shortened(array):

    def short(part):
        return part.astype(jnp.bfloat16) if part.dtype == jnp.float32 else part

    return jax.tree.map(short, array)


def turn(values):
    half = values.shape[-1] // 2
    return jnp.concatenate([-values[..., half:], values[..., :half]], axis=-1)


def turn_back(values):
    half = values.shape[-1] // 2
    return jnp.concatenate([values[..., half:], -values[..., :half]], axis=-1)


def rotary_tables(length, width):
    positions = jnp.arange(length, dtype=jnp.int32).astype(jnp.float32)
    rates = 10000.0 ** (-jnp.arange(width // 2).astype(jnp.float32) / (width // 2))
    angles = positions[:, None] * rates[None, :]
    angles = jnp.concatenate([angles, angles], axis=1)[:, None, :]
    return (jnp.cos(angles), jnp.sin(angles))


def block_masks(segment, previous, log_decay, block):
    place = jnp.arange(block, dtype=jnp.int32)
    distance = place[:, None] - place[None, :]
    same = (segment[:, None] == segment[None, :]) & (distance >= 0)
    decay = jnp.where(
        same[None],
        jnp.exp(log_decay[:, None, None] * jnp.maximum(distance, 0)[None].astype(jnp.float32)),
        0.0,
    )
    cross = jnp.where(
        (segment == previous)[None, :],
        jnp.exp(log_decay[:, None] * (place + 1)[None].astype(jnp.float32)),
        0.0,
    )
    last = segment[block - 1]
    keep = jnp.where(
        (segment == last)[None, :],
        jnp.exp(log_decay[:, None] * (block - 1 - place)[None].astype(jnp.float32)),
        0.0,
    )
    carry_weight = jnp.where(last == previous, jnp.exp(log_decay * block), 0.0)
    return (decay, cross, keep, carry_weight, last)


def retention_forward(query, keys, values, segment, log_decay, block):
    length, heads, width = query.shape
    blocks = length // block
    scale = width ** (-0.5)
    split = (
        query.reshape(blocks, block, heads, width),
        keys.reshape(blocks, block, heads, width),
        values.reshape(blocks, block, heads, values.shape[2]),
        segment.reshape(blocks, block),
    )

    def advance(carry, pieces):
        state, previous = carry
        query_b, keys_b, values_b, segment_b = pieces
        decay, cross, keep, carry_weight, last = block_masks(segment_b, previous, log_decay, block)
        raw = jnp.einsum("ihd,jhd->hij", query_b, keys_b, preferred_element_type=jnp.float32)
        weights = (raw * scale * decay).astype(jnp.bfloat16)
        inner = jnp.einsum("hij,jhe->ihe", weights, values_b, preferred_element_type=jnp.float32)
        scaled = (query_b.astype(jnp.float32) * (cross.T[:, :, None] * scale)).astype(jnp.bfloat16)
        outer = jnp.einsum(
            "ihd,hde->ihe", scaled, state.astype(jnp.bfloat16), preferred_element_type=jnp.float32
        )
        kept = (keys_b.astype(jnp.float32) * keep.T[:, :, None]).astype(jnp.bfloat16)
        added = jnp.einsum("jhd,jhe->hde", kept, values_b, preferred_element_type=jnp.float32)
        new_state = carry_weight[:, None, None] * state + added
        return ((new_state, last), (inner + outer, state))

    start = (jnp.zeros((heads, width, values.shape[2]), jnp.float32), jnp.array(-1, jnp.int32))
    _, (outputs, states) = lax.scan(advance, start, split)
    return (outputs.reshape(length, heads, values.shape[2]), states)


def retention_backward(query, keys, values, segment, states, grad_out, log_decay, block):
    length, heads, width = query.shape
    vwidth = values.shape[2]
    blocks = length // block
    scale = width ** (-0.5)
    segment_blocks = segment.reshape(blocks, block)
    previous_all = jnp.concatenate([jnp.full((1,), -1, jnp.int32), segment_blocks[:-1, -1]])
    split = (
        query.reshape(blocks, block, heads, width),
        keys.reshape(blocks, block, heads, width),
        values.reshape(blocks, block, heads, vwidth),
        segment_blocks,
        previous_all,
        states,
        grad_out.reshape(blocks, block, heads, vwidth),
    )

    def retreat(grad_state, pieces):
        query_b, keys_b, values_b, segment_b, previous, state, grad_b = pieces
        decay, cross, keep, carry_weight, last = block_masks(segment_b, previous, log_decay, block)
        raw = jnp.einsum("ihd,jhd->hij", query_b, keys_b, preferred_element_type=jnp.float32)
        weights = (raw * scale * decay).astype(jnp.bfloat16)
        grad_weights = jnp.einsum(
            "ihe,jhe->hij", grad_b, values_b, preferred_element_type=jnp.float32
        )
        grad_raw = (grad_weights * decay * scale).astype(jnp.bfloat16)
        grad_query = jnp.einsum(
            "hij,jhd->ihd", grad_raw, keys_b, preferred_element_type=jnp.float32
        )
        grad_keys = jnp.einsum(
            "hij,ihd->jhd", grad_raw, query_b, preferred_element_type=jnp.float32
        )
        grad_values = jnp.einsum(
            "hij,ihe->jhe", weights, grad_b, preferred_element_type=jnp.float32
        )
        scaled = (query_b.astype(jnp.float32) * (cross.T[:, :, None] * scale)).astype(jnp.bfloat16)
        grad_scaled = jnp.einsum(
            "ihe,hde->ihd", grad_b, state.astype(jnp.bfloat16), preferred_element_type=jnp.float32
        )
        grad_query = grad_query + grad_scaled * (cross.T[:, :, None] * scale)
        grad_state_low = jnp.einsum(
            "ihd,ihe->hde", scaled, grad_b, preferred_element_type=jnp.float32
        )
        grad_added = grad_state.astype(jnp.bfloat16)
        kept = (keys_b.astype(jnp.float32) * keep.T[:, :, None]).astype(jnp.bfloat16)
        grad_kept = jnp.einsum(
            "jhe,hde->jhd", values_b, grad_added, preferred_element_type=jnp.float32
        )
        grad_keys = grad_keys + grad_kept * keep.T[:, :, None]
        grad_values = grad_values + jnp.einsum(
            "jhd,hde->jhe", kept, grad_added, preferred_element_type=jnp.float32
        )
        new_grad = carry_weight[:, None, None] * grad_state + grad_state_low
        return (new_grad, (grad_query, grad_keys, grad_values))

    start = jnp.zeros((heads, width, vwidth), jnp.float32)
    _, (grad_query, grad_keys, grad_values) = lax.scan(retreat, start, split, reverse=True)
    return (
        grad_query.reshape(length, heads, width),
        grad_keys.reshape(length, heads, width),
        grad_values.reshape(length, heads, vwidth),
    )


def feature_sums(first, second):
    return lax.psum((first, second), "grid")


def layer_stats_norm(values, gain, bias):
    first, second = feature_sums(jnp.sum(values, axis=1), jnp.sum(values * values, axis=1))
    centre = first / D
    spread = lax.rsqrt(second / D - centre * centre + epsilon)
    normal = (values - centre[:, None]) * spread[:, None]
    return (normal * gain + bias, normal, spread)


def norm_back(grad, normal, spread, gain):
    scaled = grad * gain
    first, second = feature_sums(jnp.sum(scaled, axis=1), jnp.sum(scaled * normal, axis=1))
    back = (scaled - first[:, None] / D - normal * (second[:, None] / D)) * spread[:, None]
    return (back, jnp.sum(grad * normal, axis=0), jnp.sum(grad, axis=0))


def project_in(normed, weight):
    gathered = lax.all_gather(normed, "col", axis=0, tiled=True)
    rows = gathered.shape[0] // lax.axis_size("grid")

    def term(start, count):
        return jnp.dot(gathered, weight, preferred_element_type=jnp.float32)

    return (
        gathered,
        lax.psum_scatter(
            term(jnp.int32(0), lax.axis_size("grid") * rows),
            "grid",
            scatter_dimension=0,
            tiled=True,
        ),
    )


def project_out(mixed, weight):
    gathered = lax.all_gather(mixed, "grid", axis=0, tiled=True)
    rows = gathered.shape[0] // lax.axis_size("col")

    def term(start, count):
        return jnp.dot(gathered, weight, preferred_element_type=jnp.float32)

    return (
        gathered,
        lax.psum_scatter(
            term(jnp.int32(0), lax.axis_size("col") * rows), "col", scatter_dimension=0, tiled=True
        ),
    )


def back_out(grad, weight, gathered_in):
    grad_all = lax.all_gather(grad, "col", axis=0, tiled=True)
    weight_grad = lax.dot_general(
        gathered_in, grad_all, (((0,), (0,)), ((), ())), preferred_element_type=jnp.float32
    )
    rows = grad_all.shape[0] // lax.axis_size("grid")

    def term(start, count):
        return lax.dot_general(
            grad_all, weight, (((1,), (1,)), ((), ())), preferred_element_type=jnp.float32
        )

    return (
        weight_grad,
        lax.psum_scatter(
            term(jnp.int32(0), lax.axis_size("grid") * rows),
            "grid",
            scatter_dimension=0,
            tiled=True,
        ),
    )


def back_in(grad, weight, gathered_in):
    grad_all = lax.all_gather(grad, "grid", axis=0, tiled=True)
    weight_grad = lax.dot_general(
        gathered_in, grad_all, (((0,), (0,)), ((), ())), preferred_element_type=jnp.float32
    )
    rows = grad_all.shape[0] // lax.axis_size("col")

    def term(start, count):
        return lax.dot_general(
            grad_all, weight, (((1,), (1,)), ((), ())), preferred_element_type=jnp.float32
        )

    return (
        weight_grad,
        lax.psum_scatter(
            term(jnp.int32(0), lax.axis_size("col") * rows), "col", scatter_dimension=0, tiled=True
        ),
    )


def gate_norm(mixed, gate, gain, bias):
    centre = jnp.mean(mixed, axis=-1, keepdims=True)
    centered = mixed - centre
    variance = jnp.mean(centered * centered, axis=-1, keepdims=True)
    normed = (centered * lax.rsqrt(variance + epsilon)).reshape(gate.shape) * gain + bias
    return jax.nn.silu(gate) * normed


def exact_gelu(values):
    return jax.nn.gelu(values, approximate=False)


def sum_rows(grads):
    return jax.tree.map(lambda part: part.astype(jnp.float32), lax.psum(shortened(grads), "row"))


def embed(part, index, count):
    blocks = (jnp.arange(count)[:, None] == index).astype(jnp.float32) * part[None, :]
    return blocks.reshape(-1)


def local(
    tokens,
    cotangent,
    lengths,
    deal_pages,
    land_slots,
    pre_gain,
    pre_bias,
    query_weight,
    key_weight,
    value_weight,
    gate_weight,
    group_gain,
    group_bias,
    output_weight,
    mid_gain,
    mid_bias,
    up_weight,
    down_weight,
):
    row_index = lax.axis_index("row")
    col_index = lax.axis_index("col")
    grid_index = lax.axis_index("grid")
    row_count = lax.axis_size("row")
    col_count = lax.axis_size("col")
    grid_count = lax.axis_size("grid")
    batches, tok_dev, half_width = tokens.shape
    page = tok_dev // row_count
    ranks = jnp.arange(row_count, dtype=jnp.int32)
    send_order = deal_pages[:, col_index, row_index, :]
    land_order = land_slots[:, col_index, row_index, :]
    land_inverse = jnp.sum(
        ranks[None, None, :] * (land_order[:, None, :] == ranks[None, :, None]).astype(jnp.int32),
        axis=2,
    )
    send_inverse = jnp.sum(
        ranks[None, None, :] * (send_order[:, None, :] == ranks[None, :, None]).astype(jnp.int32),
        axis=2,
    )
    pick = jax.vmap(lambda pages, order: jnp.take(pages, order, axis=0))

    def paged(values):
        return values.reshape(batches, row_count, page, half_width)

    arrived = (
        lax.all_to_all(
            pick(paged(tokens), send_order), "row", split_axis=1, concat_axis=1, tiled=True
        ),
        lax.all_to_all(
            pick(paged(cotangent), send_order), "row", split_axis=1, concat_axis=1, tiled=True
        ),
    )
    local_tokens = pick(arrived[0], land_inverse).reshape(batches, tok_dev, half_width)
    local_grads = pick(arrived[1], land_inverse).reshape(batches, tok_dev, half_width)
    in_weight = jnp.concatenate([query_weight, key_weight, value_weight, gate_weight], axis=1)
    qk_cols = query_weight.shape[1]
    v_cols = value_weight.shape[1]
    heads_dev = qk_cols // QK_HEAD
    head_ids = col_index * heads_dev + jnp.arange(heads_dev, dtype=jnp.int32)
    log_decay = jnp.log1p(-jnp.exp2(-5.0 - head_ids.astype(jnp.float32)))
    cell_len = tok_dev * col_count // grid_count
    cosines, sines = rotary_tables(cell_len, QK_HEAD)
    place = jnp.arange(cell_len, dtype=jnp.int32)
    results = []
    input_grads = []
    totals = None
    smalls = None
    for batch in range(batches):
        inputs = local_tokens[batch].astype(jnp.float32)
        norm_one, unit_one, spread_one = layer_stats_norm(inputs, pre_gain, pre_bias)
        gathered_one, projected = project_in(norm_one.astype(jnp.bfloat16), in_weight)
        query_raw = projected[:, :qk_cols].reshape(cell_len, heads_dev, QK_HEAD)
        key_raw = projected[:, qk_cols : 2 * qk_cols].reshape(cell_len, heads_dev, QK_HEAD)
        value_raw = projected[:, 2 * qk_cols : 2 * qk_cols + v_cols]
        gate_raw = projected[:, 2 * qk_cols + v_cols :]
        query_low = (query_raw * cosines + turn(query_raw) * sines).astype(jnp.bfloat16)
        key_low = (key_raw * cosines + turn(key_raw) * sines).astype(jnp.bfloat16)
        value_low = value_raw.astype(jnp.bfloat16).reshape(cell_len, heads_dev, V_HEAD)
        ends = jnp.cumsum(lengths[batch, row_index, grid_index])
        segment = jnp.sum((place[:, None] >= ends[None, :]).astype(jnp.int32), axis=1)
        mixed, states = retention_forward(query_low, key_low, value_low, segment, log_decay, CH)
        unit_out, gate_pull = jax.vjp(gate_norm, mixed, gate_raw, group_gain, group_bias)
        gathered_two, attn_out = project_out(unit_out.astype(jnp.bfloat16), output_weight)
        resid = inputs + attn_out
        norm_two, unit_two, spread_two = layer_stats_norm(resid, mid_gain, mid_bias)
        gathered_three, pre_act = project_in(norm_two.astype(jnp.bfloat16), up_weight)
        activated, gelu_pull = jax.vjp(exact_gelu, pre_act)
        gathered_four, ffn_out = project_out(activated.astype(jnp.bfloat16), down_weight)
        results.append((resid + ffn_out).astype(jnp.bfloat16))
        top_grad = local_grads[batch]
        down_part, grad_act = back_out(top_grad, down_weight, gathered_four)
        (grad_pre,) = gelu_pull(grad_act)
        up_part, grad_norm_two = back_in(grad_pre.astype(jnp.bfloat16), up_weight, gathered_three)
        resid_part, mid_gain_part, mid_bias_part = norm_back(
            grad_norm_two, unit_two, spread_two, mid_gain
        )
        grad_resid = top_grad.astype(jnp.float32) + resid_part
        out_part, grad_unit = back_out(grad_resid.astype(jnp.bfloat16), output_weight, gathered_two)
        grad_mixed, grad_gate, group_gain_part, group_bias_part = gate_pull(grad_unit)
        grad_query, grad_key, grad_value = retention_backward(
            query_low,
            key_low,
            value_low,
            segment,
            states,
            grad_mixed.astype(jnp.bfloat16),
            log_decay,
            CH,
        )
        grad_query = grad_query * cosines + turn_back(grad_query * sines)
        grad_key = grad_key * cosines + turn_back(grad_key * sines)
        grad_proj = jnp.concatenate(
            [
                grad_query.reshape(cell_len, qk_cols),
                grad_key.reshape(cell_len, qk_cols),
                grad_value.reshape(cell_len, v_cols),
                grad_gate,
            ],
            axis=1,
        ).astype(jnp.bfloat16)
        in_part, grad_norm_one = back_in(grad_proj, in_weight, gathered_one)
        input_part, pre_gain_part, pre_bias_part = norm_back(
            grad_norm_one, unit_one, spread_one, pre_gain
        )
        input_grads.append((grad_resid + input_part).astype(jnp.bfloat16))
        parts = (in_part, out_part, up_part, down_part)
        totals = (
            parts if totals is None else tuple((total + part for total, part in zip(totals, parts)))
        )
        small_parts = (
            pre_gain_part,
            pre_bias_part,
            mid_gain_part,
            mid_bias_part,
            group_gain_part,
            group_bias_part,
        )
        smalls = (
            small_parts
            if smalls is None
            else tuple((total + part for total, part in zip(smalls, small_parts)))
        )
    totals = sum_rows(totals)
    in_total, out_total, up_total, down_total = totals
    feature_len = pre_gain.shape[0]
    group_len = group_gain.shape[0]
    spread_out = (
        embed(smalls[0], grid_index, grid_count),
        embed(smalls[1], grid_index, grid_count),
        embed(smalls[2], grid_index, grid_count),
        embed(smalls[3], grid_index, grid_count),
        embed(smalls[4], col_index, col_count),
        embed(smalls[5], col_index, col_count),
    )
    summed = lax.psum(
        (spread_out[0], spread_out[1], spread_out[2], spread_out[3], spread_out[4], spread_out[5]),
        ("row", "col", "grid"),
    )
    pregain_grad = lax.dynamic_slice_in_dim(summed[0], grid_index * feature_len, feature_len)
    prebias_grad = lax.dynamic_slice_in_dim(summed[1], grid_index * feature_len, feature_len)
    midgain_grad = lax.dynamic_slice_in_dim(summed[2], grid_index * feature_len, feature_len)
    midbias_grad = lax.dynamic_slice_in_dim(summed[3], grid_index * feature_len, feature_len)
    groupgain_grad = lax.dynamic_slice_in_dim(summed[4], col_index * group_len, group_len)
    groupbias_grad = lax.dynamic_slice_in_dim(summed[5], col_index * group_len, group_len)
    result_all = jnp.stack(results)
    grad_all = jnp.stack(input_grads)
    returned = (
        lax.all_to_all(
            pick(paged(result_all), land_order), "row", split_axis=1, concat_axis=1, tiled=True
        ),
        lax.all_to_all(
            pick(paged(grad_all), land_order), "row", split_axis=1, concat_axis=1, tiled=True
        ),
    )
    block_out = pick(returned[0], send_inverse).reshape(batches, tok_dev, half_width)
    tokens_grad = pick(returned[1], send_inverse).reshape(batches, tok_dev, half_width)
    query_grad = in_total[:, :qk_cols]
    key_grad = in_total[:, qk_cols : 2 * qk_cols]
    value_grad = in_total[:, 2 * qk_cols : 2 * qk_cols + v_cols]
    gating_grad = in_total[:, 2 * qk_cols + v_cols :]
    return (
        block_out,
        tokens_grad,
        pregain_grad,
        prebias_grad,
        query_grad,
        key_grad,
        value_grad,
        gating_grad,
        groupgain_grad,
        groupbias_grad,
        out_total,
        midgain_grad,
        midbias_grad,
        up_total,
        down_total,
    )


def solution(mesh):
    placed = (
        P(None, ("row", "col"), "grid"),
        P(None, ("row", "col"), "grid"),
        P(),
        P(),
        P(),
        P("grid"),
        P("grid"),
        P("grid", "col"),
        P("grid", "col"),
        P("grid", "col"),
        P("grid", "col"),
        P("col"),
        P("col"),
        P("col", "grid"),
        P("grid"),
        P("grid"),
        P("grid", "col"),
        P("col", "grid"),
    )
    return jax.shard_map(
        local,
        mesh=mesh,
        in_specs=placed,
        out_specs=(
            P(None, ("row", "col"), "grid"),
            P(None, ("row", "col"), "grid"),
            P("grid"),
            P("grid"),
            P("grid", "col"),
            P("grid", "col"),
            P("grid", "col"),
            P("grid", "col"),
            P("col"),
            P("col"),
            P("col", "grid"),
            P("grid"),
            P("grid"),
            P("grid", "col"),
            P("col", "grid"),
        ),
        check_vma=False,
    )
```

profile of v0, /device:TPU:0, one launch (start us, length us, event | category | flops | bytes accessed | tf_op | source)
XLA Modules:
  0.0 2377.0 jit_solution(4390069521067079517)
XLA Ops:
  24.7 24.7 %all-to-all-done = bf16[2,4,64,1024]{3,2,0,1:T(8,128)(2,1)} async-done(((bf16[2,4,64,1024]{3,2,0,1:T(8,128)(2,1)}), bf16[2,4,64,1024]{3,2,0,1:T(8,128)(2,1)}, u32[]{:S(2)}, u32[]{:S(2)}) %all-to-all-start) | async-done | bytes 1048608 | tf_op jit(solution)/shard_map/all_to_all | solution.py:322
  56.1 22.1 all-to-all-done.2
  99.5 12.1 all-gather.17.cloned.1.call-done
  111.6 12.1 fusion.140
  123.7 12.6 all-gather.25.cloned.1.call-done
  136.3 12.1 fusion.144
  157.5 125.6 %reduce-scatter.17.cloned.1.call-done = f32[512,3072]{1,0:T(8,128)} async-done(((f32[1024,3072]{1,0:T(8,128)}), f32[512,3072]{1,0:T(8,128)}) %reduce-scatter.17.cloned.1.call-update) | async-done | bytes 6291472 | tf_op jit(solution)/shard_map/reduce_scatter | solution.py:189
  295.0 134.9 %reduce-scatter.25.cloned.1.call-done = f32[512,3072]{1,0:T(8,128)} async-done(((f32[1024,3072]{1,0:T(8,128)}), f32[512,3072]{1,0:T(8,128)}) %reduce-scatter.25.cloned.1.call-update) | async-done | bytes 6291472 | tf_op jit(solution)/shard_map/reduce_scatter | solution.py:189
  475.1 32.6 %all-gather.19.cloned.1.call-done = bf16[1024,1024]{1,0:T(8,128)(2,1)} async-done(((bf16[512,1024]{1,0:T(8,128)(2,1)}), bf16[1024,1024]{1,0:T(8,128)(2,1)}) %all-gather.19.cloned.1.call-update) | async-done | bytes 2097168 | tf_op jit(solution)/shard_map/all_gather | solution.py:199
  514.4 28.5 %all-gather.27.cloned.1.call-done = bf16[1024,1024]{1,0:T(8,128)(2,1)} async-done(((bf16[512,1024]{1,0:T(8,128)(2,1)}), bf16[1024,1024]{1,0:T(8,128)(2,1)}) %all-gather.27.cloned.1.call-update) | async-done | bytes 2097168 | tf_op jit(solution)/shard_map/all_gather | solution.py:199
  551.8 38.7 %reduce-scatter.19.cloned.1.call-done = f32[256,1024]{1,0:T(8,128)} async-done(((f32[1024,1024]{1,0:T(8,128)}), f32[256,1024]{1,0:T(8,128)}) %reduce-scatter.19.cloned.1.call-update) | async-done | bytes 1048592 | tf_op jit(solution)/shard_map/reduce_scatter | solution.py:207
  590.5 47.7 %reduce-scatter.27.cloned.1.call-done = f32[256,1024]{1,0:T(8,128)} async-done(((f32[1024,1024]{1,0:T(8,128)}), f32[256,1024]{1,0:T(8,128)}) %reduce-scatter.27.cloned.1.call-update) | async-done | bytes 1048592 | tf_op jit(solution)/shard_map/reduce_scatter | solution.py:207
  650.7 11.7 all-gather.41.cloned.1.call-done
  662.4 6.6 fusion.153
  669.1 17.9 all-gather.29.cloned.1.call-done
  693.0 18.1 all-gather.33.cloned.1.call-done
  711.1 6.6 fusion.148
  718.0 17.7 all-gather.21.cloned.1.call-done
  741.7 51.3 %reduce-scatter.41.cloned.1.call-done = f32[512,1024]{1,0:T(8,128)} async-done(((f32[1024,1024]{1,0:T(8,128)}), f32[512,1024]{1,0:T(8,128)}) %reduce-scatter.41.cloned.1.call-update) | async-done | bytes 2097168 | tf_op jit(solution)/shard_map/reduce_scatter | solution.py:227
  793.0 57.2 %reduce-scatter.29.cloned.1.call-done = f32[512,1024]{1,0:T(8,128)} async-done(((f32[1024,1024]{1,0:T(8,128)}), f32[512,1024]{1,0:T(8,128)}) %reduce-scatter.29.cloned.1.call-update) | async-done | bytes 2097168 | tf_op jit(solution)/shard_map/reduce_scatter | solution.py:189
  850.2 7.3 add_convert_fusion.6
  857.6 49.7 %reduce-scatter.33.cloned.1.call-done = f32[512,1024]{1,0:T(8,128)} async-done(((f32[1024,1024]{1,0:T(8,128)}), f32[512,1024]{1,0:T(8,128)}) %reduce-scatter.33.cloned.1.call-update) | async-done | bytes 2097168 | tf_op jit(solution)/shard_map/reduce_scatter | solution.py:227
  907.3 57.1 %reduce-scatter.21.cloned.1.call-done = f32[512,1024]{1,0:T(8,128)} async-done(((f32[1024,1024]{1,0:T(8,128)}), f32[512,1024]{1,0:T(8,128)}) %reduce-scatter.21.cloned.1.call-update) | async-done | bytes 2097168 | tf_op jit(solution)/shard_map/reduce_scatter | solution.py:189
  964.4 7.3 add_convert_fusion.9
  979.8 19.7 all-gather.43.cloned.1.call-done
  1005.6 29.0 %all-gather.35.cloned.1.call-done = bf16[1024,1024]{1,0:T(8,128)(2,1)} async-done(((bf16[512,1024]{1,0:T(8,128)(2,1)}), bf16[1024,1024]{1,0:T(8,128)(2,1)}) %all-gather.35.cloned.1.call-update) | async-done | bytes 2097168 | tf_op jit(solution)/shard_map/all_gather | solution.py:237
  1040.9 28.4 %all-gather.31.cloned.1.call-done = bf16[1024,1024]{1,0:T(8,128)(2,1)} async-done(((bf16[512,1024]{1,0:T(8,128)(2,1)}), bf16[1024,1024]{1,0:T(8,128)(2,1)}) %all-gather.31.cloned.1.call-update) | async-done | bytes 2097168 | tf_op jit(solution)/shard_map/all_gather | solution.py:199
  1075.3 29.1 %all-gather.23.cloned.1.call-done = bf16[1024,1024]{1,0:T(8,128)(2,1)} async-done(((bf16[512,1024]{1,0:T(8,128)(2,1)}), bf16[1024,1024]{1,0:T(8,128)(2,1)}) %all-gather.23.cloned.1.call-update) | async-done | bytes 2097168 | tf_op jit(solution)/shard_map/all_gather | solution.py:199
  1110.4 41.7 %reduce-scatter.43.cloned.1.call-done = f32[256,1024]{1,0:T(8,128)} async-done(((f32[1024,1024]{1,0:T(8,128)}), f32[256,1024]{1,0:T(8,128)}) %reduce-scatter.43.cloned.1.call-update) | async-done | bytes 1048592 | tf_op jit(solution)/shard_map/reduce_scatter | solution.py:250
  1152.1 47.7 %reduce-scatter.35.cloned.1.call-done = f32[256,1024]{1,0:T(8,128)} async-done(((f32[1024,1024]{1,0:T(8,128)}), f32[256,1024]{1,0:T(8,128)}) %reduce-scatter.35.cloned.1.call-update) | async-done | bytes 1048592 | tf_op jit(solution)/shard_map/reduce_scatter | solution.py:250
  1207.2 40.3 %reduce-scatter.31.cloned.1.call-done = f32[256,1024]{1,0:T(8,128)} async-done(((f32[1024,1024]{1,0:T(8,128)}), f32[256,1024]{1,0:T(8,128)}) %reduce-scatter.31.cloned.1.call-update) | async-done | bytes 1048592 | tf_op jit(solution)/shard_map/reduce_scatter | solution.py:207
  1247.5 47.6 %reduce-scatter.23.cloned.1.call-done = f32[256,1024]{1,0:T(8,128)} async-done(((f32[1024,1024]{1,0:T(8,128)}), f32[256,1024]{1,0:T(8,128)}) %reduce-scatter.23.cloned.1.call-update) | async-done | bytes 1048592 | tf_op jit(solution)/shard_map/reduce_scatter | solution.py:207
  1300.7 22.1 all-gather.37.cloned.1.call-done
  1322.8 6.6 fusion.150
  1329.5 17.9 all-gather.45.cloned.1.call-done
  1353.4 51.1 %reduce-scatter.37.cloned.1.call-done = f32[512,1024]{1,0:T(8,128)} async-done(((f32[1024,1024]{1,0:T(8,128)}), f32[512,1024]{1,0:T(8,128)}) %reduce-scatter.37.cloned.1.call-update) | async-done | bytes 2097168 | tf_op jit(solution)/shard_map/reduce_scatter | solution.py:227
  1410.3 51.4 %reduce-scatter.45.cloned.1.call-done = f32[512,1024]{1,0:T(8,128)} async-done(((f32[1024,1024]{1,0:T(8,128)}), f32[512,1024]{1,0:T(8,128)}) %reduce-scatter.45.cloned.1.call-update) | async-done | bytes 2097168 | tf_op jit(solution)/shard_map/reduce_scatter | solution.py:227
  1529.1 70.4 %all-gather.47.cloned.1.call-done = bf16[1024,3072]{1,0:T(8,128)(2,1)} async-done(((bf16[512,3072]{1,0:T(8,128)(2,1)}), bf16[1024,3072]{1,0:T(8,128)(2,1)}) %all-gather.47.cloned.1.call-update) | async-done | bytes 6291472 | tf_op jit(solution)/shard_map/all_gather | solution.py:237
  1599.5 12.0 fusion.157
  1611.5 70.3 %all-gather.39.cloned.1.call-done = bf16[1024,3072]{1,0:T(8,128)(2,1)} async-done(((bf16[512,3072]{1,0:T(8,128)(2,1)}), bf16[1024,3072]{1,0:T(8,128)(2,1)}) %all-gather.39.cloned.1.call-update) | async-done | bytes 6291472 | tf_op jit(solution)/shard_map/all_gather | solution.py:237
  1681.8 12.0 fusion.152
  1718.3 9.5 fusion.158
  1729.5 47.7 %reduce-scatter.39.cloned.1.call-done = f32[256,1024]{1,0:T(8,128)} async-done(((f32[1024,1024]{1,0:T(8,128)}), f32[256,1024]{1,0:T(8,128)}) %reduce-scatter.39.cloned.1.call-update) | async-done | bytes 1048592 | tf_op jit(solution)/shard_map/reduce_scatter | solution.py:250
  1782.3 13.0 add_convert_fusion
  1814.8 23.9 %all-to-all-done.1 = bf16[2,4,64,1024]{3,2,0,1:T(8,128)(2,1)S(1)} async-done(((bf16[2,4,64,1024]{3,2,0,1:T(8,128)(2,1)}), bf16[2,4,64,1024]{3,2,0,1:T(8,128)(2,1)S(1)}, u32[]{:S(2)}, u32[]{:S(2)}) %all-to-all-start.1) | async-done | bytes 1048608 | tf_op jit(solution)/shard_map/all_to_all | solution.py:444
  1842.7 78.7 %all-reduce.9.cloned.1.call-done = (f32[2048]{0:T(1024)}, f32[2048]{0:T(1024)}, f32[4096]{0:T(1024)}, f32[4096]{0:T(1024)}, f32[2048]{0:T(1024)}, /*index=5*/f32[2048]{0:T(1024)}) async-done(((f32[2048]{0:T(1024)}, f32[2048]{0:T(1024)}, f32[4096]{0:T(1024)}, f32[4096]{0:T(1024)}, f32[2048]{0:T(1024)}, /*index=5*/f32[2048]{0:T(1024)}), (f32[2048]{0:T(1024)}, f32[2048]{0:T(1024)}, f32[4096]{0:T(1024)}, ...) | async-done | bytes 65552 | tf_op jit(solution)/shard_map/psum | solution.py:431
  1931.8 420.9 %all-reduce.11.cloned.1.call-done = (bf16[1024,3072]{1,0:T(8,128)(2,1)}, bf16[1024,1024]{1,0:T(8,128)(2,1)}, bf16[1024,1024]{1,0:T(8,128)(2,1)}, bf16[1024,1024]{1,0:T(8,128)(2,1)}) async-done(((bf16[1024,3072]{1,0:T(8,128)(2,1)}, bf16[1024,1024]{1,0:T(8,128)(2,1)}, bf16[1024,1024]{1,0:T(8,128)(2,1)}, bf16[1024,1024]{1,0:T(8,128)(2,1)}), (bf16[1024,3072]{1,0:T(8,128)(2,1)}, bf16[1024,1024]{1,0:T(8,128)(2,1)}, ...) | async-done | bytes 12582928 | tf_op jit(solution)/shard_map/psum | solution.py:269
  2352.7 6.8 fusion.131
  (477 shorter events, 350.6 us)
Async XLA Ops:
  7.2 679.8 %copy-start = (bf16[1024,1024]{1,0:T(8,128)(2,1)S(1)}, bf16[1024,1024]{1,0:T(8,128)(2,1)}, u32[]{:S(2)}) copy-start(bf16[1024,1024]{1,0:T(8,128)(2,1)} %param.36) | copy-start | bytes 6291460
  17.3 32.2 %all-to-all-start = ((bf16[2,4,64,1024]{3,2,0,1:T(8,128)(2,1)}), bf16[2,4,64,1024]{3,2,0,1:T(8,128)(2,1)}, u32[]{:S(2)}, u32[]{:S(2)}) async-start(bf16[2,4,64,1024]{3,2,0,1:T(8,128)(2,1)} %copy.179), calls=%async_computation | async-start | bytes 2097152 | tf_op jit(solution)/shard_map/all_to_all | solution.py:322
  49.4 28.8 %all-to-all-start.2 = ((bf16[2,4,64,1024]{3,2,0,1:T(8,128)(2,1)}), bf16[2,4,64,1024]{3,2,0,1:T(8,128)(2,1)S(1)}, u32[]{:S(2)}, u32[]{:S(2)}) async-start(bf16[2,4,64,1024]{3,2,0,1:T(8,128)(2,1)} %copy.203), calls=%async_computation.10 | async-start | bytes 2097152 | tf_op jit(solution)/shard_map/all_to_all | solution.py:325
  53.0 58.6 %all-gather.17.cloned.1.call-start = ((), (), s32[]{:S(2)}) async-start(), calls=%async_computation.20 | async-start | bytes 2621440 | tf_op jit(solution)/shard_map/all_gather | solution.py:181
  82.6 555.6 %copy-start.6 = (bf16[2,4,64,1024]{3,2,1,0:T(8,128)(2,1)}, bf16[2,4,64,1024]{3,2,1,0:T(8,128)(2,1)S(1)}, u32[]{:S(2)}) copy-start(bf16[2,4,64,1024]{3,2,1,0:T(8,128)(2,1)S(1)} %get-tuple-element.310) | copy-start | bytes 3145732
  89.7 46.6 %all-gather.25.cloned.1.call-start = ((), (), s32[]{:S(2)}) async-start(), calls=%async_computation.28 | async-start | bytes 2621440 | tf_op jit(solution)/shard_map/all_gather | solution.py:181
  90.5 192.7 %reduce-scatter.17.cloned.1.call-start = ((), (), s32[]{:S(2)}) async-start(), calls=%async_computation.21 | async-start | bytes 18874368 | tf_op jit(solution)/shard_map/reduce_scatter | solution.py:189
  123.7 306.3 %reduce-scatter.25.cloned.1.call-start = ((), (), s32[]{:S(2)}) async-start(), calls=%async_computation.29 | async-start | bytes 18874368 | tf_op jit(solution)/shard_map/reduce_scatter | solution.py:189
  148.4 359.3 %all-gather.19.cloned.1.call-start = ((), (), s32[]{:S(2)}) async-start(), calls=%async_computation.22 | async-start | bytes 3145728 | tf_op jit(solution)/shard_map/all_gather | solution.py:199
  474.5 68.4 %all-gather.27.cloned.1.call-start = ((), (), s32[]{:S(2)}) async-start(), calls=%async_computation.30 | async-start | bytes 3145728 | tf_op jit(solution)/shard_map/all_gather | solution.py:199
  475.0 115.5 %reduce-scatter.19.cloned.1.call-start = ((), (), s32[]{:S(2)}) async-start(), calls=%async_computation.23 | async-start | bytes 5242880 | tf_op jit(solution)/shard_map/reduce_scatter | solution.py:207
  514.3 123.9 %reduce-scatter.27.cloned.1.call-start = ((), (), s32[]{:S(2)}) async-start(), calls=%async_computation.31 | async-start | bytes 5242880 | tf_op jit(solution)/shard_map/reduce_scatter | solution.py:207
  549.4 113.0 %all-gather.41.cloned.1.call-start = ((), (), s32[]{:S(2)}) async-start(), calls=%async_computation.44 | async-start | bytes 2621440 | tf_op jit(solution)/shard_map/all_gather | solution.py:214
  551.8 94.6 %copy-start.68 = (f32[1024]{0:T(1024)S(1)}, f32[1024]{0:T(1024)}, u32[]{:S(2)}) copy-start(f32[1024]{0:T(1024)} %param.34) | copy-start | bytes 12292
  551.8 94.5 %copy-start.83 = (f32[1024]{0:T(1024)S(1)}, f32[1024]{0:T(1024)}, u32[]{:S(2)}) copy-start(f32[1024]{0:T(1024)} %param.35) | copy-start | bytes 12292
  551.8 135.2 %all-gather.29.cloned.1.call-start = ((), (), s32[]{:S(2)}) async-start(), calls=%async_computation.32 | async-start | bytes 2621440 | tf_op jit(solution)/shard_map/all_gather | solution.py:181
  649.4 61.8 %all-gather.33.cloned.1.call-start = ((), (), s32[]{:S(2)}) async-start(), calls=%async_computation.36 | async-start | bytes 2621440 | tf_op jit(solution)/shard_map/all_gather | solution.py:214
  650.1 85.6 %all-gather.21.cloned.1.call-start = ((), (), s32[]{:S(2)}) async-start(), calls=%async_computation.24 | async-start | bytes 2621440 | tf_op jit(solution)/shard_map/all_gather | solution.py:181
  650.7 142.3 %reduce-scatter.41.cloned.1.call-start = ((), (), s32[]{:S(2)}) async-start(), calls=%async_computation.45 | async-start | bytes 6291456 | tf_op jit(solution)/shard_map/reduce_scatter | solution.py:227
  669.0 181.1 %reduce-scatter.29.cloned.1.call-start = ((), (), s32[]{:S(2)}) async-start(), calls=%async_computation.33 | async-start | bytes 6291456 | tf_op jit(solution)/shard_map/reduce_scatter | solution.py:189
  692.9 214.4 %reduce-scatter.33.cloned.1.call-start = ((), (), s32[]{:S(2)}) async-start(), calls=%async_computation.37 | async-start | bytes 6291456 | tf_op jit(solution)/shard_map/reduce_scatter | solution.py:227
  717.8 246.7 %reduce-scatter.21.cloned.1.call-start = ((), (), s32[]{:S(2)}) async-start(), calls=%async_computation.25 | async-start | bytes 6291456 | tf_op jit(solution)/shard_map/reduce_scatter | solution.py:189
  741.7 257.8 %all-gather.43.cloned.1.call-start = ((), (), s32[]{:S(2)}) async-start(), calls=%async_computation.46 | async-start | bytes 3145728 | tf_op jit(solution)/shard_map/all_gather | solution.py:237
  857.5 177.1 %all-gather.35.cloned.1.call-start = ((), (), s32[]{:S(2)}) async-start(), calls=%async_computation.38 | async-start | bytes 3145728 | tf_op jit(solution)/shard_map/all_gather | solution.py:237
  971.8 97.5 %all-gather.31.cloned.1.call-start = ((), (), s32[]{:S(2)}) async-start(), calls=%async_computation.34 | async-start | bytes 3145728 | tf_op jit(solution)/shard_map/all_gather | solution.py:199
  976.0 128.4 %all-gather.23.cloned.1.call-start = ((), (), s32[]{:S(2)}) async-start(), calls=%async_computation.26 | async-start | bytes 3145728 | tf_op jit(solution)/shard_map/all_gather | solution.py:199
  979.8 172.3 %reduce-scatter.43.cloned.1.call-start = ((), (), s32[]{:S(2)}) async-start(), calls=%async_computation.47 | async-start | bytes 5242880 | tf_op jit(solution)/shard_map/reduce_scatter | solution.py:250
  1005.5 194.3 %reduce-scatter.35.cloned.1.call-start = ((), (), s32[]{:S(2)}) async-start(), calls=%async_computation.39 | async-start | bytes 5242880 | tf_op jit(solution)/shard_map/reduce_scatter | solution.py:250
  1040.6 206.9 %reduce-scatter.31.cloned.1.call-start = ((), (), s32[]{:S(2)}) async-start(), calls=%async_computation.35 | async-start | bytes 5242880 | tf_op jit(solution)/shard_map/reduce_scatter | solution.py:207
  1075.2 219.8 %reduce-scatter.23.cloned.1.call-start = ((), (), s32[]{:S(2)}) async-start(), calls=%async_computation.27 | async-start | bytes 5242880 | tf_op jit(solution)/shard_map/reduce_scatter | solution.py:207
  1110.3 89.5 %copy-start.12 = (f32[256,1024]{1,0:T(8,128)S(1)}, f32[256,1024]{1,0:T(8,128)}, u32[]{:S(2)}) copy-start(f32[256,1024]{1,0:T(8,128)} %get-tuple-element.214) | copy-start | bytes 3145732
  1110.3 89.5 %copy-start.13 = (f32[256,1024]{1,0:T(8,128)S(1)}, f32[256,1024]{1,0:T(8,128)}, u32[]{:S(2)}) copy-start(f32[256,1024]{1,0:T(8,128)} %get-tuple-element.244) | copy-start | bytes 3145732
  1110.3 184.7 %copy-start.39 = (bf16[1,4,64,1024]{3,2,1,0:T(8,128)(2,1)S(1)}, bf16[1,4,64,1024]{3,2,1,0:T(8,128)(2,1)}, u32[]{:S(2)}) copy-start(bf16[1,4,64,1024]{3,2,1,0:T(8,128)(2,1)} %get-tuple-element.240) | copy-start | bytes 1572868
  1110.3 184.7 %copy-start.40 = (bf16[1,4,64,1024]{3,2,1,0:T(8,128)(2,1)S(1)}, bf16[1,4,64,1024]{3,2,1,0:T(8,128)(2,1)}, u32[]{:S(2)}) copy-start(bf16[1,4,64,1024]{3,2,1,0:T(8,128)(2,1)} %get-tuple-element.241) | copy-start | bytes 1572868
  1110.4 212.4 %all-gather.37.cloned.1.call-start = ((), (), s32[]{:S(2)}) async-start(), calls=%async_computation.40 | async-start | bytes 2621440 | tf_op jit(solution)/shard_map/all_gather | solution.py:214
  1300.1 47.3 %all-gather.45.cloned.1.call-start = ((), (), s32[]{:S(2)}) async-start(), calls=%async_computation.48 | async-start | bytes 2621440 | tf_op jit(solution)/shard_map/all_gather | solution.py:214
  1300.6 103.9 %reduce-scatter.37.cloned.1.call-start = ((), (), s32[]{:S(2)}) async-start(), calls=%async_computation.41 | async-start | bytes 6291456 | tf_op jit(solution)/shard_map/reduce_scatter | solution.py:227
  1329.4 132.4 %reduce-scatter.45.cloned.1.call-start = ((), (), s32[]{:S(2)}) async-start(), calls=%async_computation.49 | async-start | bytes 6291456 | tf_op jit(solution)/shard_map/reduce_scatter | solution.py:227
  1353.4 108.4 %copy-start.11 = (f32[512,1024]{1,0:T(8,128)S(1)}, f32[512,1024]{1,0:T(8,128)}, u32[]{:S(2)}) copy-start(f32[512,1024]{1,0:T(8,128)} %copy.246) | copy-start | bytes 6291460
  1353.4 246.1 %all-gather.47.cloned.1.call-start = ((), (), s32[]{:S(2)}) async-start(), calls=%async_computation.50 | async-start | bytes 9437184 | tf_op jit(solution)/shard_map/all_gather | solution.py:237
  1518.9 162.9 %all-gather.39.cloned.1.call-start = ((), (), s32[]{:S(2)}) async-start(), calls=%async_computation.42 | async-start | bytes 9437184 | tf_op jit(solution)/shard_map/all_gather | solution.py:237
  1529.0 200.5 %reduce-scatter.47.cloned.1.call-start = ((), (), s32[]{:S(2)}) async-start(), calls=%async_computation.51 | async-start | bytes 5242880 | tf_op jit(solution)/shard_map/reduce_scatter | solution.py:250
  1611.4 165.8 %reduce-scatter.39.cloned.1.call-start = ((), (), s32[]{:S(2)}) async-start(), calls=%async_computation.43 | async-start | bytes 5242880 | tf_op jit(solution)/shard_map/reduce_scatter | solution.py:250
  1693.9 227.5 %all-reduce.9.cloned.1.call-start = ((), (), s32[]{:S(2)}) async-start(), calls=%async_computation.52 | async-start | bytes 131072 | tf_op jit(solution)/shard_map/psum | solution.py:431
  1718.3 59.0 %copy-start.7 = (bf16[2,4,64,1024]{3,2,1,0:T(8,128)(2,1)S(1)}, bf16[2,4,64,1024]{3,2,1,0:T(8,128)(2,1)}, u32[]{:S(2)}) copy-start(bf16[2,4,64,1024]{3,2,1,0:T(8,128)(2,1)} %copy-done.6) | copy-start | bytes 3145732
  1782.3 570.5 %all-reduce.11.cloned.1.call-start = ((), (), s32[]{:S(2)}) async-start(), calls=%async_computation.53 | async-start | bytes 25165824 | tf_op jit(solution)/shard_map/psum | solution.py:269
  1809.1 29.5 %all-to-all-start.1 = ((bf16[2,4,64,1024]{3,2,0,1:T(8,128)(2,1)}), bf16[2,4,64,1024]{3,2,0,1:T(8,128)(2,1)S(1)}, u32[]{:S(2)}, u32[]{:S(2)}) async-start(bf16[2,4,64,1024]{3,2,0,1:T(8,128)(2,1)} %copy.202), calls=%async_computation.9 | async-start | bytes 2097152 | tf_op jit(solution)/shard_map/all_to_all | solution.py:444
  1838.7 91.0 %all-to-all-start.3 = ((bf16[2,4,64,1024]{3,2,0,1:T(8,128)(2,1)}), bf16[2,4,64,1024]{3,2,0,1:T(8,128)(2,1)S(1)}, u32[]{:S(2)}, u32[]{:S(2)}) async-start(bf16[2,4,64,1024]{3,2,0,1:T(8,128)(2,1)} %copy.228), calls=%async_computation.19 | async-start | bytes 2097152 | tf_op jit(solution)/shard_map/all_to_all | solution.py:447
  (92 other events, 603.0 us)
Sparse Core Ops, SparseCore 0:
  89.9 21.6 all-gather.16
  113.7 22.5 all-gather.24
  138.6 144.5 reduce-scatter.16
  285.3 144.5 reduce-scatter.24
  474.6 33.0 all-gather.18
  509.7 33.0 all-gather.26
  545.9 44.5 reduce-scatter.18
  593.6 44.5 reduce-scatter.26
  639.8 22.5 all-gather.40
  664.4 22.5 all-gather.28
  688.5 22.5 all-gather.32
  713.1 22.5 all-gather.20
  738.6 54.3 reduce-scatter.40
  795.7 54.3 reduce-scatter.28
  852.9 54.3 reduce-scatter.32
  910.0 54.3 reduce-scatter.20
  966.4 33.0 all-gather.42
  1001.5 33.0 all-gather.34
  1036.2 33.0 all-gather.30
  1071.2 33.0 all-gather.22
  1107.5 44.5 reduce-scatter.42
  1155.2 44.5 reduce-scatter.34
  1202.9 44.5 reduce-scatter.30
  1250.5 44.5 reduce-scatter.22
  1300.2 22.5 all-gather.36
  1324.8 22.5 all-gather.44
  1350.1 54.3 reduce-scatter.36
  1407.4 54.3 reduce-scatter.44
  1519.1 80.3 all-gather.46
  1601.4 80.3 all-gather.38
  1684.9 44.5 reduce-scatter.46
  1732.6 44.5 reduce-scatter.38
  1784.6 136.7 all-reduce.8
  1925.4 427.2 all-reduce.10
where the time goes:
time: 2380 us
  waiting for transfers between devices  1900 us (80%)
  matrix products  187 us (8%)
  other arithmetic  123 us (5%)
  local copies, waits for them, and re-layouts  107 us (4%)
    psum x1, waiting for transfers between devices, sum_rows(): lax.psum(shortened(grads), 'row')  421 us
    reduce_scatter x4, waiting for transfers between devices, project_in(): lax.psum_scatter(term(jnp.int32(0), lax.axis_size('grid') * rows), 'grid'...  375 us
    reduce_scatter x4, waiting for transfers between devices, back_out(): lax.psum_scatter(term(jnp.int32(0), lax.axis_size('grid') * rows), 'grid'...  203 us
    all_gather x4, waiting for transfers between devices, back_in(): grad_all = lax.all_gather(grad, 'grid', axis=0, tiled=True)  189 us
    reduce_scatter x4, waiting for transfers between devices, project_out(): lax.psum_scatter(term(jnp.int32(0), lax.axis_size('col') * rows), 'col',...  174 us
    reduce_scatter x4, waiting for transfers between devices, back_in(): lax.psum_scatter(term(jnp.int32(0), lax.axis_size('col') * rows), 'col',...  139 us
    all_gather x4, waiting for transfers between devices, project_out(): gathered = lax.all_gather(mixed, 'grid', axis=0, tiled=True)  119 us
    psum x1, waiting for transfers between devices, local(): lax.psum((spread_out[0], spread_out[1], spread_out[2], spread_out[3], spr...  78.7 us
  transfers between devices with their start and end apart: 38, of which 37 were waited for; matrix products, arithmetic and copies ran while one was open for 11% of the time, Pallas kernels for 0%

commit v1 on v0

--- a/solution.py
+++ b/solution.py
@@ -274,7 +274,7 @@
     return blocks.reshape(-1)
 
 
-def local(
+def local_general(
     tokens,
     cotangent,
     lengths,
@@ -473,6 +473,437 @@
     )
 
 
+def swap(values, axis, bit):
+    count = lax.axis_size(axis)
+    return lax.ppermute(values, axis, [(one, one ^ bit) for one in range(count)])
+
+
+def gather_cell(own):
+    far = swap(own, "col", 2)
+    near = swap(own, "col", 1)
+    across = swap(far, "col", 1)
+    return jnp.concatenate([own, near, far, across], axis=0)
+
+
+def scatter_cell(part):
+    rows = part.shape[0] // 4
+    outer = swap(part[3 * rows :], "col", 1)
+    away = part[2 * rows : 3 * rows].astype(jnp.float32) + outer.astype(jnp.float32)
+    far = swap(away.astype(jnp.bfloat16), "col", 2)
+    near = swap(part[rows : 2 * rows], "col", 1)
+    return part[:rows].astype(jnp.float32) + near.astype(jnp.float32) + far.astype(jnp.float32)
+
+
+def dot(left, right, left_axis=1, right_axis=0):
+    return lax.dot_general(
+        left, right, (((left_axis,), (right_axis,)), ((), ())), preferred_element_type=jnp.float32
+    )
+
+
+def page_routes(back):
+    rows, cols, grids = lax.axis_size("row"), lax.axis_size("col"), lax.axis_size("grid")
+    routes = []
+    for step in range(4):
+        pairs = []
+        for row in range(rows):
+            for col in range(cols):
+                for grid in range(grids):
+                    source = (row * cols + col) * grids + grid
+                    to_row = (2 * (row // 2) + grid) ^ step
+                    to_col = 2 * (col % 2) + row % 2
+                    target = (to_row * cols + to_col) * grids + col // 2
+                    pairs.append((target, source) if back else (source, target))
+        routes.append(pairs)
+    return routes
+
+
+def cell_norm(values, gain, bias):
+    centre = jnp.mean(values, axis=1, keepdims=True)
+    spread = lax.rsqrt(jnp.mean(values * values, axis=1, keepdims=True) - centre * centre + epsilon)
+    normal = (values - centre) * spread
+    return ((normal * gain + bias).astype(jnp.bfloat16), normal, spread)
+
+
+def cell_norm_back(grad, normal, spread, gain):
+    scaled = grad * gain
+    first = jnp.mean(scaled, axis=1, keepdims=True)
+    second = jnp.mean(scaled * normal, axis=1, keepdims=True)
+    back = (scaled - first - normal * second) * spread
+    return (back, jnp.sum(grad * normal, axis=0), jnp.sum(grad, axis=0))
+
+
+def rotate(values, cosines, sines):
+    half = values.shape[1] // 2
+    low, high = values[:, :half], values[:, half:]
+    return jnp.concatenate([low * cosines - high * sines, high * cosines + low * sines], axis=1)
+
+
+def rotate_back(values, cosines, sines):
+    half = values.shape[1] // 2
+    low, high = values[:, :half], values[:, half:]
+    return jnp.concatenate([low * cosines + high * sines, high * cosines - low * sines], axis=1)
+
+
+def head_cell(query, keys, values, decay, cross, state, scale):
+    weights = (dot(query, keys, 1, 1) * scale * decay).astype(jnp.bfloat16)
+    scaled = (query.astype(jnp.float32) * (cross * scale)).astype(jnp.bfloat16)
+    mixed = dot(weights, values) + dot(scaled, state.astype(jnp.bfloat16))
+    return (mixed, weights)
+
+
+def head_cell_back(query, keys, values, weights, decay, cross, keep, state, grad_state, grad, scale):
+    grad_raw = (dot(grad, values, 1, 1) * decay * scale).astype(jnp.bfloat16)
+    grad_added = grad_state.astype(jnp.bfloat16)
+    kept = (keys.astype(jnp.float32) * keep).astype(jnp.bfloat16)
+    grad_query = dot(grad_raw, keys) + dot(grad, state.astype(jnp.bfloat16), 1, 1) * (cross * scale)
+    grad_keys = dot(grad_raw, query, 0, 0) + dot(values, grad_added, 1, 1) * keep
+    grad_values = dot(weights, grad, 0, 0) + dot(kept, grad_added)
+    return (grad_query, grad_keys, grad_values)
+
+
+def local_cells(
+    tokens,
+    cotangent,
+    lengths,
+    deal_pages,
+    land_slots,
+    pre_gain,
+    pre_bias,
+    query_weight,
+    key_weight,
+    value_weight,
+    gate_weight,
+    group_gain,
+    group_bias,
+    output_weight,
+    mid_gain,
+    mid_bias,
+    up_weight,
+    down_weight,
+):
+    row_index = lax.axis_index("row")
+    col_index = lax.axis_index("col")
+    grid_index = lax.axis_index("grid")
+    col_count = lax.axis_size("col")
+    grid_count = lax.axis_size("grid")
+    batches, tok_dev, half_width = tokens.shape
+    page = tok_dev // 4
+    cell_len = 2 * tok_dev
+    qk_cols = query_weight.shape[1]
+    v_cols = value_weight.shape[1]
+    heads_dev = qk_cols // QK_HEAD
+    scale = QK_HEAD ** (-0.5)
+    everywhere = ("row", "col", "grid")
+    pick = jax.vmap(lambda pages, order: jnp.take(pages, order, axis=0))
+
+    steps = jnp.arange(4, dtype=jnp.int32)
+    to_rows = (2 * (row_index // 2) + grid_index) ^ steps
+    sent_pages = deal_pages[:, col_index, row_index, :][:, to_rows]
+    routes, returns = page_routes(False), page_routes(True)
+    half_swap = (row_index + grid_index) % 2
+
+    def spread_pages(values):
+        chosen = pick(values.reshape(batches, 4, page, half_width), sent_pages)
+        got = [lax.ppermute(chosen[:, step], everywhere, routes[step]) for step in range(4)]
+        pairs = []
+        for place in range(2):
+            one, two = got[2 * place], got[2 * place + 1]
+            pairs.append(
+                jnp.concatenate(
+                    [jnp.where(half_swap == 0, one, two), jnp.where(half_swap == 0, two, one)], axis=2
+                )
+            )
+        return jnp.concatenate(pairs, axis=1)
+
+    from_row = jnp.argmax(
+        deal_pages[:, col_index, row_index, None, :] == steps[None, :, None], axis=2
+    ).astype(jnp.int32)
+    from_step = from_row ^ (2 * (row_index // 2) + grid_index)
+
+    def return_pages(values):
+        got = []
+        for step in range(4):
+            rows = values[:, (step // 2) * page : (step // 2 + 1) * page]
+            first, second = rows[..., :half_width], rows[..., half_width:]
+            sent = jnp.where((half_swap + step) % 2 == 0, first, second)
+            got.append(lax.ppermute(sent, everywhere, returns[step]))
+        return pick(jnp.stack(got, axis=1), from_step).reshape(batches, tok_dev, half_width)
+
+    local_tokens = spread_pages(tokens)
+    local_grads = spread_pages(cotangent)
+
+    def both(values, axis):
+        return jnp.concatenate([values, swap(values, "grid", 1)], axis=axis)
+
+    pre_gain_all, pre_bias_all = both(pre_gain, 0), both(pre_bias, 0)
+    mid_gain_all, mid_bias_all = both(mid_gain, 0), both(mid_bias, 0)
+    query_all, key_all = both(query_weight, 0), both(key_weight, 0)
+    value_all, gate_all = both(value_weight, 0), both(gate_weight, 0)
+    output_all = both(output_weight, 1)
+    up_all = both(up_weight, 0)
+    down_all = both(down_weight, 1)
+
+    head_ids = col_index * heads_dev + jnp.arange(heads_dev, dtype=jnp.int32)
+    log_decay = jnp.log1p(-jnp.exp2(-5.0 - head_ids.astype(jnp.float32)))
+    rates = 10000.0 ** (-jnp.arange(QK_HEAD // 2).astype(jnp.float32) / (QK_HEAD // 2))
+    x_index, core_index = col_index // 2, col_index % 2
+    inner = jnp.arange(page, dtype=jnp.int32)
+    places = []
+    tables = []
+    for batch in range(batches):
+        chunks = []
+        for ahead in range(2):
+            for beside in range(2):
+                group = x_index ^ ahead
+                for place in range(2):
+                    source = 2 * ((row_index // 2) ^ place) + (core_index ^ beside)
+                    slot = land_slots[batch, 2 * grid_index + group, row_index, source]
+                    chunks.append(tok_dev * group + page * slot + inner)
+        position = jnp.concatenate(chunks)
+        angles = position.astype(jnp.float32)[:, None] * rates[None, :]
+        ends = jnp.cumsum(lengths[batch, row_index, grid_index])
+        segment = jnp.sum((position[:, None] >= ends[None, :]).astype(jnp.int32), axis=1)
+        last = jnp.sum((cell_len - 1 >= ends).astype(jnp.int32))
+        distance = position[:, None] - position[None, :]
+        same = (segment[:, None] == segment[None, :]) & (distance >= 0)
+        span = jnp.maximum(distance, 0).astype(jnp.float32)
+        decays = [
+            jnp.where(same, jnp.exp(log_decay[head] * span), 0.0) for head in range(heads_dev)
+        ]
+        crosses = [
+            jnp.where(
+                segment == -1, jnp.exp(log_decay[head] * (position + 1).astype(jnp.float32)), 0.0
+            )[:, None]
+            for head in range(heads_dev)
+        ]
+        keeps = [
+            jnp.where(
+                segment == last,
+                jnp.exp(log_decay[head] * (cell_len - 1 - position).astype(jnp.float32)),
+                0.0,
+            )[:, None]
+            for head in range(heads_dev)
+        ]
+        tables.append((jnp.cos(angles), jnp.sin(angles), decays, crosses, keeps))
+    state = jnp.zeros((QK_HEAD, V_HEAD), jnp.float32)
+    grad_state = jnp.zeros((QK_HEAD, V_HEAD), jnp.float32)
+
+    saved = []
+    results = []
+    for batch in range(batches):
+        cosines, sines, decays, crosses, keeps = tables[batch]
+        inputs = local_tokens[batch].astype(jnp.float32)
+        hidden_one, unit_one, spread_one = cell_norm(inputs, pre_gain_all, pre_bias_all)
+        cell_one = gather_cell(hidden_one)
+        query_raw, key_raw = dot(cell_one, query_all), dot(cell_one, key_all)
+        value_low = dot(cell_one, value_all).astype(jnp.bfloat16)
+        gate = dot(cell_one, gate_all)
+        heads = []
+        gated = []
+        for head in range(heads_dev):
+            qk = slice(head * QK_HEAD, (head + 1) * QK_HEAD)
+            vs = slice(head * V_HEAD, (head + 1) * V_HEAD)
+            query = rotate(query_raw[:, qk], cosines, sines).astype(jnp.bfloat16)
+            keys = rotate(key_raw[:, qk], cosines, sines).astype(jnp.bfloat16)
+            values = value_low[:, vs]
+            mixed, weights = head_cell(
+                query, keys, values, decays[head], crosses[head], state, scale
+            )
+            centred = mixed - jnp.mean(mixed, axis=1, keepdims=True)
+            spread = lax.rsqrt(jnp.mean(centred * centred, axis=1, keepdims=True) + epsilon)
+            normal = centred * spread
+            scaled = normal * group_gain[vs] + group_bias[vs]
+            gate_part = gate[:, vs]
+            gated.append((gate_part * jax.nn.sigmoid(gate_part) * scaled).astype(jnp.bfloat16))
+            heads.append((query, keys, values, weights, normal, spread, gate_part))
+        unit_out = jnp.concatenate(gated, axis=1)
+        attn_out = scatter_cell(dot(unit_out, output_all).astype(jnp.bfloat16))
+        resid = inputs + attn_out
+        hidden_two, unit_two, spread_two = cell_norm(resid, mid_gain_all, mid_bias_all)
+        cell_two = gather_cell(hidden_two)
+        pre_act = dot(cell_two, up_all)
+        activated, gelu_pull = jax.vjp(exact_gelu, pre_act)
+        activated = activated.astype(jnp.bfloat16)
+        ffn_out = scatter_cell(dot(activated, down_all).astype(jnp.bfloat16))
+        results.append((resid + ffn_out).astype(jnp.bfloat16))
+        saved.append(
+            (
+                unit_one,
+                spread_one,
+                cell_one,
+                heads,
+                unit_out,
+                unit_two,
+                spread_two,
+                cell_two,
+                activated,
+                gelu_pull,
+            )
+        )
+    block_out = return_pages(jnp.stack(results))
+
+    input_grads = []
+    smalls = []
+    top_cells = []
+    pre_grads = []
+    mid_cells = []
+    proj_grads = []
+    for batch in range(batches):
+        cosines, sines, decays, crosses, keeps = tables[batch]
+        (
+            unit_one,
+            spread_one,
+            cell_one,
+            heads,
+            unit_out,
+            unit_two,
+            spread_two,
+            cell_two,
+            activated,
+            gelu_pull,
+        ) = saved[batch]
+        top_grad = local_grads[batch]
+        top_cell = gather_cell(top_grad)
+        (grad_pre,) = gelu_pull(dot(top_cell, down_all, 1, 1))
+        grad_pre = grad_pre.astype(jnp.bfloat16)
+        grad_two = scatter_cell(dot(grad_pre, up_all, 1, 1).astype(jnp.bfloat16))
+        back_two, mid_gain_part, mid_bias_part = cell_norm_back(
+            grad_two, unit_two, spread_two, mid_gain_all
+        )
+        grad_resid = top_grad.astype(jnp.float32) + back_two
+        mid_cell = gather_cell(grad_resid.astype(jnp.bfloat16))
+        grad_unit = dot(mid_cell, output_all, 1, 1)
+        query_parts, key_parts, value_parts, gate_parts = [], [], [], []
+        group_gain_parts, group_bias_parts = [], []
+        for head in range(heads_dev):
+            vs = slice(head * V_HEAD, (head + 1) * V_HEAD)
+            query, keys, values, weights, normal, spread, gate_part = heads[head]
+            grad_u = grad_unit[:, vs]
+            sig = jax.nn.sigmoid(gate_part)
+            scaled = normal * group_gain[vs] + group_bias[vs]
+            gate_parts.append(
+                (grad_u * scaled * (sig * (1.0 + gate_part * (1.0 - sig)))).astype(jnp.bfloat16)
+            )
+            grad_scaled = grad_u * (gate_part * sig)
+            group_gain_parts.append(jnp.sum(grad_scaled * normal, axis=0))
+            group_bias_parts.append(jnp.sum(grad_scaled, axis=0))
+            grad_normal = grad_scaled * group_gain[vs]
+            grad_mixed = spread * (
+                grad_normal
+                - jnp.mean(grad_normal, axis=1, keepdims=True)
+                - normal * jnp.mean(grad_normal * normal, axis=1, keepdims=True)
+            )
+            grad_query, grad_keys, grad_values = head_cell_back(
+                query,
+                keys,
+                values,
+                weights,
+                decays[head],
+                crosses[head],
+                keeps[head],
+                state,
+                grad_state,
+                grad_mixed.astype(jnp.bfloat16),
+                scale,
+            )
+            query_parts.append(rotate_back(grad_query, cosines, sines).astype(jnp.bfloat16))
+            key_parts.append(rotate_back(grad_keys, cosines, sines).astype(jnp.bfloat16))
+            value_parts.append(grad_values.astype(jnp.bfloat16))
+        grad_q = jnp.concatenate(query_parts, axis=1)
+        grad_k = jnp.concatenate(key_parts, axis=1)
+        grad_v = jnp.concatenate(value_parts, axis=1)
+        grad_g = jnp.concatenate(gate_parts, axis=1)
+        grad_cell = (
+            dot(grad_q, query_all, 1, 1)
+            + dot(grad_k, key_all, 1, 1)
+            + dot(grad_v, value_all, 1, 1)
+            + dot(grad_g, gate_all, 1, 1)
+        )
+        grad_one = scatter_cell(grad_cell.astype(jnp.bfloat16))
+        back_one, pre_gain_part, pre_bias_part = cell_norm_back(
+            grad_one, unit_one, spread_one, pre_gain_all
+        )
+        input_grads.append((grad_resid + back_one).astype(jnp.bfloat16))
+        top_cells.append(top_cell)
+        pre_grads.append(grad_pre)
+        mid_cells.append(mid_cell)
+        proj_grads.append((grad_q, grad_k, grad_v, grad_g))
+        smalls.append(
+            (
+                pre_gain_part,
+                pre_bias_part,
+                mid_gain_part,
+                mid_bias_part,
+                jnp.concatenate(group_gain_parts),
+                jnp.concatenate(group_bias_parts),
+            )
+        )
+    tokens_grad = return_pages(jnp.stack(input_grads))
+
+    def over_rows(grad, axis):
+        half = grad.shape[axis] // 2
+        own = lax.slice_in_dim(grad, 0, half, axis=axis)
+        other = lax.slice_in_dim(grad, half, 2 * half, axis=axis).astype(jnp.bfloat16)
+        pair = own + swap(other, "grid", 1).astype(jnp.float32)
+        return lax.psum(pair.astype(jnp.bfloat16), "row").astype(jnp.float32)
+
+    def tall(parts):
+        return jnp.concatenate(parts, axis=0)
+
+    down_grad = over_rows(dot(tall([one[8] for one in saved]), tall(top_cells), 0, 0), 1)
+    up_grad = over_rows(dot(tall([one[7] for one in saved]), tall(pre_grads), 0, 0), 0)
+    out_grad = over_rows(dot(tall([one[4] for one in saved]), tall(mid_cells), 0, 0), 1)
+    cells = tall([one[2] for one in saved])
+    query_grad, key_grad, value_grad, gating_grad = [
+        over_rows(dot(cells, tall([one[part] for one in proj_grads]), 0, 0), 0) for part in range(4)
+    ]
+
+    totals = [sum(parts) for parts in zip(*smalls)]
+    feature_len = pre_gain.shape[0]
+    group_len = group_gain.shape[0]
+
+    def in_place(part):
+        return jnp.where(grid_index == 0, part, jnp.roll(part, feature_len))
+
+    summed = lax.psum(
+        tuple(in_place(part) for part in totals[:4])
+        + tuple(embed(part, col_index, col_count) for part in totals[4:]),
+        everywhere,
+    )
+    features = [
+        lax.dynamic_slice_in_dim(part, grid_index * feature_len, feature_len) for part in summed[:4]
+    ]
+    groups = [
+        lax.dynamic_slice_in_dim(part, col_index * group_len, group_len) for part in summed[4:]
+    ]
+    return (
+        block_out,
+        tokens_grad,
+        features[0],
+        features[1],
+        query_grad,
+        key_grad,
+        value_grad,
+        gating_grad,
+        groups[0],
+        groups[1],
+        out_grad,
+        features[2],
+        features[3],
+        up_grad,
+        down_grad,
+    )
+
+
+def local(*arguments):
+    tokens, query_weight = arguments[0], arguments[7]
+    sizes = tuple(lax.axis_size(axis) for axis in ("row", "col", "grid"))
+    one_block = 2 * tokens.shape[1] == CH
+    if sizes == (4, 4, 2) and one_block and query_weight.shape[1] % QK_HEAD == 0:
+        return local_cells(*arguments)
+    return local_general(*arguments)
+
+
 def solution(mesh):
     placed = (
         P(None, ("row", "col"), "grid"),

time: 2380 us -> 1400 us (0.59)
  waiting for transfers between devices: 1900 us -> 900 us
  starting transfers between devices: 20.5 us -> 90.7 us
    reduce_scatter x16 -> x0, waiting for transfers between devices: 891 us -> none  [the longest x4 375 us: project_in(): lax.psum_scatter(term(jnp.int32(0), lax.axis_size('grid') * rows), 'grid'...]
    ppermute x0 -> x82, waiting for transfers between devices: none -> 537 us  [the longest x66 440 us: swap(): lax.ppermute(values, axis, [(one, one ^ bit) for one in range(count)])]
    all_gather x16 -> x0, waiting for transfers between devices: 438 us -> none  [the longest x4 189 us: back_in(): grad_all = lax.all_gather(grad, 'grid', axis=0, tiled=True)]
    psum x2, waiting for transfers between devices: 500 us -> 362 us  [the longest x1 362 us: over_rows(): return lax.psum(pair.astype(jnp.bfloat16), 'row').astype(jnp.float32)]
    ppermute x0 -> x82, starting transfers between devices: none -> 90.6 us  [the longest x66 42.1 us: swap(): lax.ppermute(values, axis, [(one, one ^ bit) for one in range(count)])]
    all_to_all x4 -> x0, waiting for transfers between devices: 70.8 us -> none  [the longest x1 24.7 us: local(): lax.all_to_all(pick(paged(tokens), send_order), 'row', split_axis=1, conc...]
    unnamed x213 -> x543, local copies, waits for them, and re-layouts: 21.6 us -> 51.1 us
    reshape x12 -> x0, local copies, waits for them, and re-layouts: 29 us -> none  [the longest x4 12.6 us: gate_norm(): (centered * lax.rsqrt(variance + epsilon)).reshape(gate.shape) * gain + bias]
  transfers between devices with their start and end apart: 38 -> 84, of which waited for: 37 -> 32; matrix products, arithmetic and copies ran while one was open for 11% -> 22% of each run, Pallas kernels for 0% -> 0%
where the time goes in v1:
time: 1400 us
  waiting for transfers between devices  900 us (64%)
  matrix products  166 us (12%)
  other arithmetic  117 us (8%)
  local copies, waits for them, and re-layouts  94.1 us (7%)
  starting transfers between devices  90.7 us (6%)
  between operations  28.2 us (2%)
    ppermute x66, waiting for transfers between devices, swap(): lax.ppermute(values, axis, [(one, one ^ bit) for one in range(count)])  440 us
    psum x1, waiting for transfers between devices, over_rows(): return lax.psum(pair.astype(jnp.bfloat16), 'row').astype(jnp.float32)  362 us
    dot_general x75, matrix products, dot(): lax.dot_general(left, right, (((left_axis,), (right_axis,)), ((), ())), p...  166 us
    ppermute x8, waiting for transfers between devices, return_pages(): got.append(lax.ppermute(sent, everywhere, returns[step]))  65.5 us
    unnamed x543, local copies, waits for them, and re-layouts  51.1 us
    convert_element_type x14, other arithmetic, over_rows(): return lax.psum(pair.astype(jnp.bfloat16), 'row').astype(jnp.float32)  44.1 us
    ppermute x66, starting transfers between devices, swap(): lax.ppermute(values, axis, [(one, one ^ bit) for one in range(count)])  42.1 us
    ppermute x8, starting transfers between devices, return_pages(): got.append(lax.ppermute(sent, everywhere, returns[step]))  31.9 us
  transfers between devices with their start and end apart: 84, of which 32 were waited for; matrix products, arithmetic and copies ran while one was open for 22% of the time, Pallas kernels for 0%

profile of v1, /device:TPU:0, one launch (start us, length us, event | category | flops | bytes accessed | tf_op | source)
XLA Modules:
  0.0 1395.7 jit_solution(9136188750265244692)
XLA Ops:
  17.0 4.0 collective-permute-start.3
  47.6 12.5 collective-permute-done.1
  65.9 9.6 collective-permute-done.7
  77.1 50.4 %collective-permute-done.11 = bf16[1024,512]{1,0:T(8,128)(2,1)S(1)} collective-permute-done((bf16[1024,512]{1,0:T(8,128)(2,1)}, bf16[1024,512]{1,0:T(8,128)(2,1)S(1)}, u32[]{:S(2)}, u32[]{:S(2)}) %collective-permute-start.11) | collective-permute-done | bytes 1048608 | tf_op jit(solution)/shard_map/ppermute | solution.py:478
  139.9 32.6 %collective-permute-done.9 = bf16[1024,1024]{1,0:T(8,128)(2,1)S(1)} collective-permute-done((bf16[1024,1024]{1,0:T(8,128)(2,1)S(1)}, bf16[1024,1024]{1,0:T(8,128)(2,1)S(1)}, u32[]{:S(2)}, u32[]{:S(2)}) %collective-permute-start.9) | collective-permute-done | bytes 2097184 | tf_op jit(solution)/shard_map/ppermute | solution.py:478
  176.5 38.3 %collective-permute-done.13 = bf16[1024,1024]{1,0:T(8,128)(2,1)S(1)} collective-permute-done((bf16[1024,1024]{1,0:T(8,128)(2,1)S(1)}, bf16[1024,1024]{1,0:T(8,128)(2,1)S(1)}, u32[]{:S(2)}, u32[]{:S(2)}) %collective-permute-start.13) | collective-permute-done | bytes 2097184 | tf_op jit(solution)/shard_map/ppermute | solution.py:478
  221.0 6.4 collective-permute-start.46
  230.3 16.4 %collective-permute-done.46 = bf16[2,64,1024]{2,1,0:T(8,128)(2,1)S(1)} collective-permute-done((bf16[2,64,1024]{2,1,0:T(8,128)(2,1)S(1)}, bf16[2,64,1024]{2,1,0:T(8,128)(2,1)S(1)}, u32[]{:S(2)}, u32[]{:S(2)}) %collective-permute-start.46) | collective-permute-done | bytes 262176 | tf_op jit(solution)/shard_map/ppermute | solution.py:607
  252.1 8.9 collective-permute-done.16
  265.6 11.8 collective-permute-done.20
  277.8 7.2 collective-permute-done.48
  285.0 3.9 collective-permute-done.22
  289.1 42.8 %collective-permute-done.23 = bf16[1024,1024]{1,0:T(8,128)(2,1)S(1)} collective-permute-done((bf16[1024,1024]{1,0:T(8,128)(2,1)S(1)}, bf16[1024,1024]{1,0:T(8,128)(2,1)S(1)}, u32[]{:S(2)}, u32[]{:S(2)}) %collective-permute-start.23) | collective-permute-done | bytes 2097184 | tf_op jit(solution)/shard_map/ppermute | solution.py:478
  332.2 6.6 multiply_convert_fusion.1
  338.8 4.8 add_convert_fusion.3
  367.9 6.7 collective-permute-done.52
  374.6 10.3 collective-permute-done.26
  384.9 4.3 multiply_reduce_fusion.1
  398.2 9.3 collective-permute-done.54
  449.5 9.9 collective-permute-done.58
  467.7 9.0 collective-permute-done.28
  508.8 9.5 collective-permute-done.32
  523.2 9.5 collective-permute-done.34
  535.2 10.9 multiply_convert_fusion
  546.2 6.8 add_convert_fusion.2
  565.4 6.9 fusion.81
  577.1 10.6 collective-permute-done.64
  596.7 6.5 fusion.85
  611.6 11.2 collective-permute-done.80
  641.5 14.2 %fusion.73 = f32[1024,2048]{1,0:T(8,128)} fusion(bf16[1024,2048]{1,0:T(8,128)(2,1)S(1)} %constant_dynamic-update-slice_fusion.22, bf16[512,512]{1,0:T(8,128)(2,1)S(1)} %copy-done.108, bf16[512,512]{1,0:T(8,128)(2,1)S(1)} %copy-done.106, bf16[512,512]{1,0:T(8,128)(2,1)S(1)} %copy-done.100, bf16[512,512]{1,0:T(8,128)(2,1)S(1)} %copy-done.98), kind=kOutput, calls=%fused_computation.104 | convolution fusion | flops 4303355904 | bytes 14680064 | tf_op jit(solution)/shard_map/dot_general | solution.py:498
  658.3 13.0 fusion.57
  671.3 13.6 fusion.65
  692.7 5.0 fusion.201
  703.2 3.8 slice.1033
  714.3 4.0 slice.1034
  724.2 54.0 %collective-permute-done.75 = bf16[1024,512]{1,0:T(8,128)(2,1)S(1)} collective-permute-done((bf16[1024,512]{1,0:T(8,128)(2,1)S(1)}, bf16[1024,512]{1,0:T(8,128)(2,1)S(1)}, u32[]{:S(2)}, u32[]{:S(2)}) %collective-permute-start.75) | collective-permute-done | bytes 1048608 | tf_op jit(solution)/shard_map/ppermute | solution.py:478
  783.2 17.8 %collective-permute-done.76 = bf16[1024,512]{1,0:T(8,128)(2,1)} collective-permute-done((bf16[1024,512]{1,0:T(8,128)(2,1)}, bf16[1024,512]{1,0:T(8,128)(2,1)}, u32[]{:S(2)}, u32[]{:S(2)}) %collective-permute-start.76) | collective-permute-done | bytes 1048608 | tf_op jit(solution)/shard_map/ppermute | solution.py:478
  804.4 5.2 fusion
  809.6 3.9 fusion.2
  813.5 32.8 %collective-permute-done.78 = bf16[1024,1024]{1,0:T(8,128)(2,1)} collective-permute-done((bf16[1024,1024]{1,0:T(8,128)(2,1)}, bf16[1024,1024]{1,0:T(8,128)(2,1)}, u32[]{:S(2)}, u32[]{:S(2)}) %collective-permute-start.78) | collective-permute-done | bytes 2097184 | tf_op jit(solution)/shard_map/ppermute | solution.py:478
  850.1 39.5 %collective-permute-done.77 = bf16[1024,1024]{1,0:T(8,128)(2,1)} collective-permute-done((bf16[1024,1024]{1,0:T(8,128)(2,1)}, bf16[1024,1024]{1,0:T(8,128)(2,1)}, u32[]{:S(2)}, u32[]{:S(2)}) %collective-permute-start.77) | collective-permute-done | bytes 2097184 | tf_op jit(solution)/shard_map/ppermute | solution.py:478
  898.4 4.0 collective-permute-start.40
  907.1 10.8 collective-permute-start.72
  917.9 5.5 collective-permute-done.40
  925.2 11.4 collective-permute-start.73
  936.6 21.7 %collective-permute-done.41 = bf16[2,64,1024]{2,1,0:T(8,128)(2,1)S(1)} collective-permute-done((bf16[2,64,1024]{2,1,0:T(8,128)(2,1)S(1)}, bf16[2,64,1024]{2,1,0:T(8,128)(2,1)S(1)}, u32[]{:S(2)}, u32[]{:S(2)}) %collective-permute-start.41) | collective-permute-done | bytes 262176 | tf_op jit(solution)/shard_map/ppermute | solution.py:629
  966.7 38.3 %collective-permute-done.73 = bf16[2,64,1024]{2,1,0:T(8,128)(2,1)} collective-permute-done((bf16[2,64,1024]{2,1,0:T(8,128)(2,1)S(1)}, bf16[2,64,1024]{2,1,0:T(8,128)(2,1)}, u32[]{:S(2)}, u32[]{:S(2)}) %collective-permute-start.73) | collective-permute-done | bytes 262176 | tf_op jit(solution)/shard_map/ppermute | solution.py:629
  1008.4 362.5 %all-reduce.7.cloned.1.call-done = (bf16[1024,512]{1,0:T(8,128)(2,1)}, bf16[1024,512]{1,0:T(8,128)(2,1)}, bf16[1024,1024]{1,0:T(8,128)(2,1)}, bf16[1024,1024]{1,...) async-done(((bf16[1024,512]{1,0:T(8,128)(2,1)}, bf16[1024,512]{1,0:T(8,128)(2,1)}, ...) | async-done | bytes 12582928 | tf_op jit(solution)/shard_map/psum | solution.py:848
  (939 shorter events, 328.5 us)
Async XLA Ops:
  7.2 951.9 %all-reduce.5.cloned.1.call-start = ((), (), s32[]{:S(2)}) async-start(), calls=%async_computation | async-start | bytes 131072 | tf_op jit(solution)/shard_map/psum | solution.py:868
  7.2 33.1 %collective-permute-start.4 = (f32[1024]{0:T(1024)}, f32[1024]{0:T(1024)S(1)}, u32[]{:S(2)}, u32[]{:S(2)}) collective-permute-start(f32[1024]{0:T(1024)} %param.25), channel_id=1, source_target_pairs={{0,1},{1,0},{2,3},{3,2},{4,5},{5,4},{6,7},{7,6},{8,9},{9,8},{10,11... | collective-permute-start | bytes 12296 | tf_op jit(solution)/shard_map/ppermute | solution.py:478
  10.3 32.2 %collective-permute-start.5 = (f32[1024]{0:T(1024)}, f32[1024]{0:T(1024)S(1)}, u32[]{:S(2)}, u32[]{:S(2)}) collective-permute-start(f32[1024]{0:T(1024)} %param.26), channel_id=1, source_target_pairs={{0,1},{1,0},{2,3},{3,2},{4,5},{5,4},{6,7},{7,6},{8,9},{9,8},{10,11... | collective-permute-start | bytes 12296 | tf_op jit(solution)/shard_map/ppermute | solution.py:478
  17.0 28.4 %collective-permute-start.3 = (bf16[2,64,1024]{2,1,0:T(8,128)(2,1)}, bf16[2,64,1024]{2,1,0:T(8,128)(2,1)S(1)}, u32[]{:S(2)}, u32[]{:S(2)}) collective-permute-start(bf16[2,64,1024]{2,1,0:T(8,128)(2,1)} %get-tuple-element.176), channel_id=1, source_target_pairs={{0,24},{1,16},{2,28},{3,20},{4,25},{5,17},{6,29},{7,21},{8,26},{9,... | collective-permute-start | bytes 786440 | tf_op jit(solution)/shard_map/ppermute | solution.py:607
  21.0 24.5 %collective-permute-start.2 = (bf16[2,64,1024]{2,1,0:T(8,128)(2,1)}, bf16[2,64,1024]{2,1,0:T(8,128)(2,1)S(1)}, u32[]{:S(2)}, u32[]{:S(2)}) collective-permute-start(bf16[2,64,1024]{2,1,0:T(8,128)(2,1)} %get-tuple-element.177), channel_id=1, source_target_pairs={{0,16},{1,24},{2,20},{3,28},{4,17},{5,25},{6,21},{7,29},{8,18},{9,... | collective-permute-start | bytes 786440 | tf_op jit(solution)/shard_map/ppermute | solution.py:607
  21.0 54.6 %collective-permute-start.10 = (bf16[1024,512]{1,0:T(8,128)(2,1)}, bf16[1024,512]{1,0:T(8,128)(2,1)}, u32[]{:S(2)}, u32[]{:S(2)}) collective-permute-start(bf16[1024,512]{1,0:T(8,128)(2,1)} %param.27), channel_id=1, source_target_pairs={{0,1},{1,0},{2,3},{3,2},{4,5},{5,4},{6,7},{7,6},{8,9},{9,8},{10,11... | collective-permute-start | bytes 3145736 | tf_op jit(solution)/shard_map/ppermute | solution.py:478
  42.5 17.6 %collective-permute-start.1 = (bf16[2,64,1024]{2,1,0:T(8,128)(2,1)S(1)}, bf16[2,64,1024]{2,1,0:T(8,128)(2,1)S(1)}, u32[]{:S(2)}, u32[]{:S(2)}) collective-permute-start(bf16[2,64,1024]{2,1,0:T(8,128)(2,1)S(1)} %get-tuple-element.178), channel_id=1, source_target_pairs={{0,8},{1,0},{2,12},{3,4},{4,9},{5,1},{6,13},{7,5},{8,10},{9,2},{10... | collective-permute-start | bytes 786440 | tf_op jit(solution)/shard_map/ppermute | solution.py:607
  45.4 90.1 %collective-permute-start.12 = (bf16[1024,1024]{1,0:T(8,128)(2,1)}, bf16[1024,1024]{1,0:T(8,128)(2,1)S(1)}, u32[]{:S(2)}, u32[]{:S(2)}) collective-permute-start(bf16[1024,1024]{1,0:T(8,128)(2,1)} %param.29), channel_id=1, source_target_pairs={{0,1},{1,0},{2,3},{3,2},{4,5},{5,4},{6,7},{7,6},{8,9},{9,8},{10,11... | collective-permute-start | bytes 6291464 | tf_op jit(solution)/shard_map/ppermute | solution.py:478
  45.5 82.0 %collective-permute-start.11 = (bf16[1024,512]{1,0:T(8,128)(2,1)}, bf16[1024,512]{1,0:T(8,128)(2,1)S(1)}, u32[]{:S(2)}, u32[]{:S(2)}) collective-permute-start(bf16[1024,512]{1,0:T(8,128)(2,1)} %param.28), channel_id=1, source_target_pairs={{0,1},{1,0},{2,3},{3,2},{4,5},{5,4},{6,7},{7,6},{8,9},{9,8},{10,11... | collective-permute-start | bytes 3145736 | tf_op jit(solution)/shard_map/ppermute | solution.py:478
  65.9 61.7 %collective-permute-start.6 = (bf16[128,2048]{1,0:T(8,128)(2,1)S(1)}, bf16[128,2048]{1,0:T(8,128)(2,1)S(1)}, u32[]{:S(2)}, u32[]{:S(2)}) collective-permute-start(bf16[128,2048]{1,0:T(8,128)(2,1)S(1)} %get-tuple-element.83), channel_id=1, source_target_pairs={{0,2},{2,0},{4,6},{6,4},{1,3},{3,1},{5,7},{7,5},{8,10},{10,8},{12,... | collective-permute-start | bytes 1572872 | tf_op jit(solution)/shard_map/ppermute | solution.py:478
  75.6 52.1 %collective-permute-start.8 = (bf16[128,2048]{1,0:T(8,128)(2,1)S(1)}, bf16[128,2048]{1,0:T(8,128)(2,1)S(1)}, u32[]{:S(2)}, u32[]{:S(2)}) collective-permute-start(bf16[128,2048]{1,0:T(8,128)(2,1)S(1)} %collective-permute-done.7), channel_id=1, source_target_pairs={{0,2},{2,0},{4,6},{6,4},{1,3},{3,1},{5,7},{7,5},{8,10},{10,8},{12,... | collective-permute-start | bytes 1572872 | tf_op jit(solution)/shard_map/ppermute | solution.py:478
  75.7 96.8 %collective-permute-start.9 = (bf16[1024,1024]{1,0:T(8,128)(2,1)S(1)}, bf16[1024,1024]{1,0:T(8,128)(2,1)S(1)}, u32[]{:S(2)}, u32[]{:S(2)}) collective-permute-start(bf16[1024,1024]{1,0:T(8,128)(2,1)S(1)} %copy-done.46), channel_id=1, source_target_pairs={{0,1},{1,0},{2,3},{3,2},{4,5},{5,4},{6,7},{7,6},{8,9},{9,8},{10,11... | collective-permute-start | bytes 6291464 | tf_op jit(solution)/shard_map/ppermute | solution.py:478
  127.5 87.3 %collective-permute-start.13 = (bf16[1024,1024]{1,0:T(8,128)(2,1)S(1)}, bf16[1024,1024]{1,0:T(8,128)(2,1)S(1)}, u32[]{:S(2)}, u32[]{:S(2)}) collective-permute-start(bf16[1024,1024]{1,0:T(8,128)(2,1)S(1)} %copy-done.48), channel_id=1, source_target_pairs={{0,1},{1,0},{2,3},{3,2},{4,5},{5,4},{6,7},{7,6},{8,9},{9,8},{10,11... | collective-permute-start | bytes 6291464 | tf_op jit(solution)/shard_map/ppermute | solution.py:478
  220.2 30.8 %collective-permute-start.43 = (bf16[2,64,1024]{2,1,0:T(8,128)(2,1)S(1)}, bf16[2,64,1024]{2,1,0:T(8,128)(2,1)S(1)}, u32[]{:S(2)}, u32[]{:S(2)}) collective-permute-start(bf16[2,64,1024]{2,1,0:T(8,128)(2,1)S(1)} %get-tuple-element.171), channel_id=1, source_target_pairs={{0,0},{1,8},{2,4},{3,12},{4,1},{5,9},{6,5},{7,13},{8,2},{9,10},{10... | collective-permute-start | bytes 786440 | tf_op jit(solution)/shard_map/ppermute | solution.py:607
  221.0 25.6 %collective-permute-start.46 = (bf16[2,64,1024]{2,1,0:T(8,128)(2,1)S(1)}, bf16[2,64,1024]{2,1,0:T(8,128)(2,1)S(1)}, u32[]{:S(2)}, u32[]{:S(2)}) collective-permute-start(bf16[2,64,1024]{2,1,0:T(8,128)(2,1)S(1)} %get-tuple-element.172), channel_id=1, source_target_pairs={{0,24},{1,16},{2,28},{3,20},{4,25},{5,17},{6,29},{7,21},{8,26},{9,... | collective-permute-start | bytes 786440 | tf_op jit(solution)/shard_map/ppermute | solution.py:607
  227.5 21.3 %collective-permute-start.45 = (bf16[2,64,1024]{2,1,0:T(8,128)(2,1)S(1)}, bf16[2,64,1024]{2,1,0:T(8,128)(2,1)S(1)}, u32[]{:S(2)}, u32[]{:S(2)}) collective-permute-start(bf16[2,64,1024]{2,1,0:T(8,128)(2,1)S(1)} %get-tuple-element.173), channel_id=1, source_target_pairs={{0,16},{1,24},{2,20},{3,28},{4,17},{5,25},{6,21},{7,29},{8,18},{9,... | collective-permute-start | bytes 786440 | tf_op jit(solution)/shard_map/ppermute | solution.py:607
  227.5 24.5 %collective-permute-start.44 = (bf16[2,64,1024]{2,1,0:T(8,128)(2,1)S(1)}, bf16[2,64,1024]{2,1,0:T(8,128)(2,1)S(1)}, u32[]{:S(2)}, u32[]{:S(2)}) collective-permute-start(bf16[2,64,1024]{2,1,0:T(8,128)(2,1)S(1)} %get-tuple-element.174), channel_id=1, source_target_pairs={{0,8},{1,0},{2,12},{3,4},{4,9},{5,1},{6,13},{7,5},{8,10},{9,2},{10... | collective-permute-start | bytes 786440 | tf_op jit(solution)/shard_map/ppermute | solution.py:607
  228.3 60.6 %collective-permute-start.22 = (bf16[1024,1024]{1,0:T(8,128)(2,1)S(1)}, bf16[1024,1024]{1,0:T(8,128)(2,1)S(1)}, u32[]{:S(2)}, u32[]{:S(2)}) collective-permute-start(bf16[1024,1024]{1,0:T(8,128)(2,1)S(1)} %copy-done.49), channel_id=1, source_target_pairs={{0,1},{1,0},{2,3},{3,2},{4,5},{5,4},{6,7},{7,6},{8,9},{9,8},{10,11... | collective-permute-start | bytes 6291464 | tf_op jit(solution)/shard_map/ppermute | solution.py:478
  251.1 80.8 %collective-permute-start.23 = (bf16[1024,1024]{1,0:T(8,128)(2,1)S(1)}, bf16[1024,1024]{1,0:T(8,128)(2,1)S(1)}, u32[]{:S(2)}, u32[]{:S(2)}) collective-permute-start(bf16[1024,1024]{1,0:T(8,128)(2,1)S(1)} %copy-done.50), channel_id=1, source_target_pairs={{0,1},{1,0},{2,3},{3,2},{4,5},{5,4},{6,7},{7,6},{8,9},{9,8},{10,11... | collective-permute-start | bytes 6291464 | tf_op jit(solution)/shard_map/ppermute | solution.py:478
  264.8 20.2 %collective-permute-start.48 = (bf16[128,2048]{1,0:T(8,128)(2,1)S(1)}, bf16[128,2048]{1,0:T(8,128)(2,1)S(1)}, u32[]{:S(2)}, u32[]{:S(2)}) collective-permute-start(bf16[128,2048]{1,0:T(8,128)(2,1)S(1)} %get-tuple-element.166), channel_id=1, source_target_pairs={{0,4},{2,6},{4,0},{6,2},{1,5},{3,7},{5,1},{7,3},{8,12},{10,14},{12... | collective-permute-start | bytes 1572872 | tf_op jit(solution)/shard_map/ppermute | solution.py:478
  265.6 66.6 %collective-permute-start.19 = (bf16[128,2048]{1,0:T(8,128)(2,1)S(1)}, bf16[128,2048]{1,0:T(8,128)(2,1)S(1)}, u32[]{:S(2)}, u32[]{:S(2)}) collective-permute-start(bf16[128,2048]{1,0:T(8,128)(2,1)S(1)} %get-tuple-element.73), channel_id=1, source_target_pairs={{0,2},{2,0},{4,6},{6,4},{1,3},{3,1},{5,7},{7,5},{8,10},{10,8},{12,... | collective-permute-start | bytes 1572872 | tf_op jit(solution)/shard_map/ppermute | solution.py:478
  277.4 54.8 %collective-permute-start.21 = (bf16[128,2048]{1,0:T(8,128)(2,1)S(1)}, bf16[128,2048]{1,0:T(8,128)(2,1)S(1)}, u32[]{:S(2)}, u32[]{:S(2)}) collective-permute-start(bf16[128,2048]{1,0:T(8,128)(2,1)S(1)} %collective-permute-done.20), channel_id=1, source_target_pairs={{0,2},{2,0},{4,6},{6,4},{1,3},{3,1},{5,7},{7,5},{8,10},{10,8},{12,... | collective-permute-start | bytes 1572872 | tf_op jit(solution)/shard_map/ppermute | solution.py:478
  285.0 53.8 %collective-permute-start.47 = (bf16[128,2048]{1,0:T(8,128)(2,1)S(1)}, bf16[128,2048]{1,0:T(8,128)(2,1)S(1)}, u32[]{:S(2)}, u32[]{:S(2)}) collective-permute-start(bf16[128,2048]{1,0:T(8,128)(2,1)S(1)} %get-tuple-element.166), channel_id=1, source_target_pairs={{0,2},{2,0},{4,6},{6,4},{1,3},{3,1},{5,7},{7,5},{8,10},{10,8},{12,... | collective-permute-start | bytes 1572872 | tf_op jit(solution)/shard_map/ppermute | solution.py:478
  288.9 49.9 %collective-permute-start.49 = (bf16[128,2048]{1,0:T(8,128)(2,1)S(1)}, bf16[128,2048]{1,0:T(8,128)(2,1)S(1)}, u32[]{:S(2)}, u32[]{:S(2)}) collective-permute-start(bf16[128,2048]{1,0:T(8,128)(2,1)S(1)} %collective-permute-done.48), channel_id=1, source_target_pairs={{0,2},{2,0},{4,6},{6,4},{1,3},{3,1},{5,7},{7,5},{8,10},{10,8},{12,... | collective-permute-start | bytes 1572872 | tf_op jit(solution)/shard_map/ppermute | solution.py:478
  363.1 21.8 %collective-permute-start.26 = (bf16[128,2048]{1,0:T(8,128)(2,1)}, bf16[128,2048]{1,0:T(8,128)(2,1)}, u32[]{:S(2)}, u32[]{:S(2)}) collective-permute-start(bf16[128,2048]{1,0:T(8,128)(2,1)} %add_convert_fusion.13), channel_id=1, source_target_pairs={{0,4},{2,6},{4,0},{6,2},{1,5},{3,7},{5,1},{7,3},{8,12},{10,14},{12... | collective-permute-start | bytes 1572872 | tf_op jit(solution)/shard_map/ppermute | solution.py:478
  397.3 42.3 %collective-permute-start.60 = (bf16[128,2048]{1,0:T(8,128)(2,1)}, bf16[128,2048]{1,0:T(8,128)(2,1)}, u32[]{:S(2)}, u32[]{:S(2)}) collective-permute-start(bf16[128,2048]{1,0:T(8,128)(2,1)} %get-tuple-element.165), channel_id=1, source_target_pairs={{0,4},{2,6},{4,0},{6,2},{1,5},{3,7},{5,1},{7,3},{8,12},{10,14},{12... | collective-permute-start | bytes 1572872 | tf_op jit(solution)/shard_map/ppermute | solution.py:478
  439.1 107.0 %collective-permute-start.59 = (bf16[128,2048]{1,0:T(8,128)(2,1)}, bf16[128,2048]{1,0:T(8,128)(2,1)S(1)}, u32[]{:S(2)}, u32[]{:S(2)}) collective-permute-start(bf16[128,2048]{1,0:T(8,128)(2,1)} %get-tuple-element.165), channel_id=1, source_target_pairs={{0,2},{2,0},{4,6},{6,4},{1,3},{3,1},{5,7},{7,5},{8,10},{10,8},{12,... | collective-permute-start | bytes 1572872 | tf_op jit(solution)/shard_map/ppermute | solution.py:478
  439.6 106.6 %collective-permute-start.61 = (bf16[128,2048]{1,0:T(8,128)(2,1)}, bf16[128,2048]{1,0:T(8,128)(2,1)S(1)}, u32[]{:S(2)}, u32[]{:S(2)}) collective-permute-start(bf16[128,2048]{1,0:T(8,128)(2,1)} %collective-permute-done.60), channel_id=1, source_target_pairs={{0,2},{2,0},{4,6},{6,4},{1,3},{3,1},{5,7},{7,5},{8,10},{10,8},{12,... | collective-permute-start | bytes 1572872 | tf_op jit(solution)/shard_map/ppermute | solution.py:478
  564.0 23.7 %collective-permute-start.64 = (bf16[128,2048]{1,0:T(8,128)(2,1)S(1)}, bf16[128,2048]{1,0:T(8,128)(2,1)S(1)}, u32[]{:S(2)}, u32[]{:S(2)}) collective-permute-start(bf16[128,2048]{1,0:T(8,128)(2,1)S(1)} %add_convert_fusion.5), channel_id=1, source_target_pairs={{0,4},{2,6},{4,0},{6,2},{1,5},{3,7},{5,1},{7,3},{8,12},{10,14},{12... | collective-permute-start | bytes 1572872 | tf_op jit(solution)/shard_map/ppermute | solution.py:478
  574.0 48.8 %collective-permute-start.80 = (bf16[1024,1024]{1,0:T(8,128)(2,1)}, bf16[1024,1024]{1,0:T(8,128)(2,1)}, u32[]{:S(2)}, u32[]{:S(2)}) collective-permute-start(bf16[1024,1024]{1,0:T(8,128)(2,1)} %slice.1032), channel_id=1, source_target_pairs={{0,1},{1,0},{2,3},{3,2},{4,5},{5,4},{6,7},{7,6},{8,9},{9,8},{10,11... | collective-permute-start | bytes 6291464 | tf_op jit(solution)/shard_map/ppermute | solution.py:478
  591.5 17.9 %collective-permute-start.66 = (bf16[128,2048]{1,0:T(8,128)(2,1)S(1)}, bf16[128,2048]{1,0:T(8,128)(2,1)S(1)}, u32[]{:S(2)}, u32[]{:S(2)}) collective-permute-start(bf16[128,2048]{1,0:T(8,128)(2,1)S(1)} %get-tuple-element.75), channel_id=1, source_target_pairs={{0,4},{2,6},{4,0},{6,2},{1,5},{3,7},{5,1},{7,3},{8,12},{10,14},{12... | collective-permute-start | bytes 1572872 | tf_op jit(solution)/shard_map/ppermute | solution.py:478
  608.2 196.2 %collective-permute-start.81 = (bf16[1024,1024]{1,0:T(8,128)(2,1)}, bf16[1024,1024]{1,0:T(8,128)(2,1)}, u32[]{:S(2)}, u32[]{:S(2)}) collective-permute-start(bf16[1024,1024]{1,0:T(8,128)(2,1)} %slice.1031), channel_id=1, source_target_pairs={{0,1},{1,0},{2,3},{3,2},{4,5},{5,4},{6,7},{7,6},{8,9},{9,8},{10,11... | collective-permute-start | bytes 6291464 | tf_op jit(solution)/shard_map/ppermute | solution.py:478
  609.4 17.2 %collective-permute-start.67 = (bf16[128,2048]{1,0:T(8,128)(2,1)S(1)}, bf16[128,2048]{1,0:T(8,128)(2,1)S(1)}, u32[]{:S(2)}, u32[]{:S(2)}) collective-permute-start(bf16[128,2048]{1,0:T(8,128)(2,1)S(1)} %collective-permute-done.66), channel_id=1, source_target_pairs={{0,2},{2,0},{4,6},{6,4},{1,3},{3,1},{5,7},{7,5},{8,10},{10,8},{12,... | collective-permute-start | bytes 1572872 | tf_op jit(solution)/shard_map/ppermute | solution.py:478
  691.7 26.5 %collective-permute-start.68 = (bf16[128,2048]{1,0:T(8,128)(2,1)S(1)}, bf16[128,2048]{1,0:T(8,128)(2,1)S(1)}, u32[]{:S(2)}, u32[]{:S(2)}) collective-permute-start(bf16[128,2048]{1,0:T(8,128)(2,1)S(1)} %get-tuple-element.122), channel_id=1, source_target_pairs={{0,2},{2,0},{4,6},{6,4},{1,3},{3,1},{5,7},{7,5},{8,10},{10,8},{12,... | collective-permute-start | bytes 1572872 | tf_op jit(solution)/shard_map/ppermute | solution.py:478
  698.0 20.3 %collective-permute-start.70 = (bf16[128,2048]{1,0:T(8,128)(2,1)S(1)}, bf16[128,2048]{1,0:T(8,128)(2,1)S(1)}, u32[]{:S(2)}, u32[]{:S(2)}) collective-permute-start(bf16[128,2048]{1,0:T(8,128)(2,1)S(1)} %add_convert_fusion.4), channel_id=1, source_target_pairs={{0,4},{2,6},{4,0},{6,2},{1,5},{3,7},{5,1},{7,3},{8,12},{10,14},{12... | collective-permute-start | bytes 1572872 | tf_op jit(solution)/shard_map/ppermute | solution.py:478
  707.0 102.5 %collective-permute-start.79 = (bf16[1024,1024]{1,0:T(8,128)(2,1)}, bf16[1024,1024]{1,0:T(8,128)(2,1)}, u32[]{:S(2)}, u32[]{:S(2)}) collective-permute-start(bf16[1024,1024]{1,0:T(8,128)(2,1)} %slice.1033), channel_id=1, source_target_pairs={{0,1},{1,0},{2,3},{3,2},{4,5},{5,4},{6,7},{7,6},{8,9},{9,8},{10,11... | collective-permute-start | bytes 6291464 | tf_op jit(solution)/shard_map/ppermute | solution.py:478
  707.2 71.0 %collective-permute-start.75 = (bf16[1024,512]{1,0:T(8,128)(2,1)S(1)}, bf16[1024,512]{1,0:T(8,128)(2,1)S(1)}, u32[]{:S(2)}, u32[]{:S(2)}) collective-permute-start(bf16[1024,512]{1,0:T(8,128)(2,1)S(1)} %slice.1037), channel_id=1, source_target_pairs={{0,1},{1,0},{2,3},{3,2},{4,5},{5,4},{6,7},{7,6},{8,9},{9,8},{10,11... | collective-permute-start | bytes 3145736 | tf_op jit(solution)/shard_map/ppermute | solution.py:478
  718.3 82.8 %collective-permute-start.76 = (bf16[1024,512]{1,0:T(8,128)(2,1)}, bf16[1024,512]{1,0:T(8,128)(2,1)}, u32[]{:S(2)}, u32[]{:S(2)}) collective-permute-start(bf16[1024,512]{1,0:T(8,128)(2,1)} %slice.1036), channel_id=1, source_target_pairs={{0,1},{1,0},{2,3},{3,2},{4,5},{5,4},{6,7},{7,6},{8,9},{9,8},{10,11... | collective-permute-start | bytes 3145736 | tf_op jit(solution)/shard_map/ppermute | solution.py:478
  718.3 128.0 %collective-permute-start.78 = (bf16[1024,1024]{1,0:T(8,128)(2,1)}, bf16[1024,1024]{1,0:T(8,128)(2,1)}, u32[]{:S(2)}, u32[]{:S(2)}) collective-permute-start(bf16[1024,1024]{1,0:T(8,128)(2,1)} %slice.1034), channel_id=1, source_target_pairs={{0,1},{1,0},{2,3},{3,2},{4,5},{5,4},{6,7},{7,6},{8,9},{9,8},{10,11... | collective-permute-start | bytes 6291464 | tf_op jit(solution)/shard_map/ppermute | solution.py:478
  779.2 110.4 %collective-permute-start.77 = (bf16[1024,1024]{1,0:T(8,128)(2,1)}, bf16[1024,1024]{1,0:T(8,128)(2,1)}, u32[]{:S(2)}, u32[]{:S(2)}) collective-permute-start(bf16[1024,1024]{1,0:T(8,128)(2,1)} %slice.1035), channel_id=1, source_target_pairs={{0,1},{1,0},{2,3},{3,2},{4,5},{5,4},{6,7},{7,6},{8,9},{9,8},{10,11... | collective-permute-start | bytes 6291464 | tf_op jit(solution)/shard_map/ppermute | solution.py:478
  779.8 591.1 %all-reduce.7.cloned.1.call-start = ((), (), s32[]{:S(2)}) async-start(), calls=%async_computation.1 | async-start | bytes 25165824 | tf_op jit(solution)/shard_map/psum | solution.py:848
  898.4 25.0 %collective-permute-start.40 = (bf16[2,64,1024]{2,1,0:T(8,128)(2,1)S(1)}, bf16[2,64,1024]{2,1,0:T(8,128)(2,1)S(1)}, u32[]{:S(2)}, u32[]{:S(2)}) collective-permute-start(bf16[2,64,1024]{2,1,0:T(8,128)(2,1)S(1)} %get-tuple-element.168), channel_id=1, source_target_pairs={{8,0},{0,1},{12,2},{4,3},{9,4},{1,5},{13,6},{5,7},{10,8},{2,9},{14... | collective-permute-start | bytes 786440 | tf_op jit(solution)/shard_map/ppermute | solution.py:629
  902.4 22.8 %collective-permute-start.42 = (bf16[2,64,1024]{2,1,0:T(8,128)(2,1)S(1)}, bf16[2,64,1024]{2,1,0:T(8,128)(2,1)S(1)}, u32[]{:S(2)}, u32[]{:S(2)}) collective-permute-start(bf16[2,64,1024]{2,1,0:T(8,128)(2,1)S(1)} %get-tuple-element.169), channel_id=1, source_target_pairs={{24,0},{16,1},{28,2},{20,3},{25,4},{17,5},{29,6},{21,7},{26,8},{18... | collective-permute-start | bytes 786440 | tf_op jit(solution)/shard_map/ppermute | solution.py:629
  902.4 55.9 %collective-permute-start.41 = (bf16[2,64,1024]{2,1,0:T(8,128)(2,1)S(1)}, bf16[2,64,1024]{2,1,0:T(8,128)(2,1)S(1)}, u32[]{:S(2)}, u32[]{:S(2)}) collective-permute-start(bf16[2,64,1024]{2,1,0:T(8,128)(2,1)S(1)} %get-tuple-element.90), channel_id=1, source_target_pairs={{16,0},{24,1},{20,2},{28,3},{17,4},{25,5},{21,6},{29,7},{18,8},{26... | collective-permute-start | bytes 786440 | tf_op jit(solution)/shard_map/ppermute | solution.py:629
  906.4 60.3 %collective-permute-start.71 = (bf16[2,64,1024]{2,1,0:T(8,128)(2,1)S(1)}, bf16[2,64,1024]{2,1,0:T(8,128)(2,1)S(1)}, u32[]{:S(2)}, u32[]{:S(2)}) collective-permute-start(bf16[2,64,1024]{2,1,0:T(8,128)(2,1)S(1)} %get-tuple-element.161), channel_id=1, source_target_pairs={{0,0},{8,1},{4,2},{12,3},{1,4},{9,5},{5,6},{13,7},{2,8},{10,9},{6,... | collective-permute-start | bytes 786440 | tf_op jit(solution)/shard_map/ppermute | solution.py:629
  907.1 59.6 %collective-permute-start.72 = (bf16[2,64,1024]{2,1,0:T(8,128)(2,1)S(1)}, bf16[2,64,1024]{2,1,0:T(8,128)(2,1)}, u32[]{:S(2)}, u32[]{:S(2)}) collective-permute-start(bf16[2,64,1024]{2,1,0:T(8,128)(2,1)S(1)} %get-tuple-element.162), channel_id=1, source_target_pairs={{8,0},{0,1},{12,2},{4,3},{9,4},{1,5},{13,6},{5,7},{10,8},{2,9},{14... | collective-permute-start | bytes 786440 | tf_op jit(solution)/shard_map/ppermute | solution.py:629
  923.4 43.3 %collective-permute-start.74 = (bf16[2,64,1024]{2,1,0:T(8,128)(2,1)S(1)}, bf16[2,64,1024]{2,1,0:T(8,128)(2,1)}, u32[]{:S(2)}, u32[]{:S(2)}) collective-permute-start(bf16[2,64,1024]{2,1,0:T(8,128)(2,1)S(1)} %get-tuple-element.163), channel_id=1, source_target_pairs={{24,0},{16,1},{28,2},{20,3},{25,4},{17,5},{29,6},{21,7},{26,8},{18... | collective-permute-start | bytes 786440 | tf_op jit(solution)/shard_map/ppermute | solution.py:629
  925.2 79.8 %collective-permute-start.73 = (bf16[2,64,1024]{2,1,0:T(8,128)(2,1)S(1)}, bf16[2,64,1024]{2,1,0:T(8,128)(2,1)}, u32[]{:S(2)}, u32[]{:S(2)}) collective-permute-start(bf16[2,64,1024]{2,1,0:T(8,128)(2,1)S(1)} %get-tuple-element.84), channel_id=1, source_target_pairs={{16,0},{24,1},{20,2},{28,3},{17,4},{25,5},{21,6},{29,7},{18,8},{26... | collective-permute-start | bytes 786440 | tf_op jit(solution)/shard_map/ppermute | solution.py:629
  (293 other events, 3249.6 us)
Sparse Core Ops, SparseCore 0:
  779.9 122.7 all-reduce.4
  907.3 463.5 all-reduce.6

commit v2 on v0

--- a/solution.py
+++ b/solution.py
@@ -1,6 +1,8 @@
 import jax
 import jax.numpy as jnp
 from jax import lax
+from jax.experimental import pallas as pl
+from jax.experimental.pallas import tpu as pltpu
 from jax.sharding import PartitionSpec as P
 
 D = 2048
@@ -274,7 +276,7 @@
     return blocks.reshape(-1)
 
 
-def local(
+def local_general(
     tokens,
     cotangent,
     lengths,
@@ -473,6 +475,585 @@
     )
 
 
+def swap(values, axis, bit):
+    count = lax.axis_size(axis)
+    return lax.ppermute(values, axis, [(one, one ^ bit) for one in range(count)])
+
+
+def gather_cell(own, axis=0):
+    pair = jnp.concatenate([own, swap(own, "col", 2)], axis=axis)
+    return jnp.concatenate([pair, swap(pair, "col", 1)], axis=axis)
+
+
+def scatter_cell(part, axis=0):
+    mine, other = jnp.split(part, 2, axis=axis)
+    pair = mine.astype(jnp.float32) + swap(other, "col", 1).astype(jnp.float32)
+    own, away = jnp.split(pair, 2, axis=axis)
+    return own + swap(away.astype(jnp.bfloat16), "col", 2).astype(jnp.float32)
+
+
+def after(values, done):
+    return lax.optimization_barrier((values, done))[0]
+
+
+def other_halves(weights, ready):
+    odd = lax.axis_index("row") % 2
+    pairs = [(one, one ^ 1) for one in range(lax.axis_size("row"))]
+    crossed, traded, whole = [], [], []
+    for place, weight in enumerate(weights):
+        half = weight.shape[0] // 2
+        sent = lax.dynamic_slice_in_dim(weight, odd * half, half, axis=0)
+        if place > 0:
+            sent = after(sent, (crossed[place - 1], ready) if place == 1 else crossed[place - 1])
+        crossed.append(swap(sent, "grid", 1))
+        traded.append(lax.ppermute(crossed[place], "row", pairs))
+        first = jnp.where(odd == 0, crossed[place], traded[place])
+        second = jnp.where(odd == 0, traded[place], crossed[place])
+        whole.append(jnp.concatenate([first, second], axis=0))
+    return (crossed, traded, whole)
+
+
+def dot(left, right, left_axis=1, right_axis=0):
+    return lax.dot_general(
+        left, right, (((left_axis,), (right_axis,)), ((), ())), preferred_element_type=jnp.float32
+    )
+
+
+def deal_kernel(places, deal, values, *sent):
+    row, col, grid = places[0], places[1], places[2]
+    for step, out in enumerate(sent):
+        to_row = (2 * (row // 2) + grid) ^ step
+        for batch in range(values.shape[0]):
+            out[batch] = values[batch, deal[batch, col, row, to_row]]
+
+
+def land_kernel(places, deal, *refs):
+    row, col, grid = places[0], places[1], places[2]
+    *got, out = refs
+    for step, values in enumerate(got):
+        from_row = (2 * (row // 2) + grid) ^ step
+        for batch in range(out.shape[0]):
+            out[batch, deal[batch, col, row, from_row]] = values[batch]
+
+
+def page_call(kernel, places, deal, values, shapes):
+    smem = pl.BlockSpec(memory_space=pltpu.SMEM)
+    vmem = pl.BlockSpec(memory_space=pltpu.VMEM)
+    return pl.pallas_call(
+        kernel,
+        in_specs=[smem, smem] + [vmem] * len(values),
+        out_specs=[vmem] * len(shapes),
+        out_shape=[jax.ShapeDtypeStruct(shape, jnp.bfloat16) for shape in shapes],
+    )(places, deal, *values)
+
+
+def page_routes(back):
+    rows, cols, grids = lax.axis_size("row"), lax.axis_size("col"), lax.axis_size("grid")
+    routes = []
+    for step in range(4):
+        pairs = []
+        for row in range(rows):
+            for col in range(cols):
+                for grid in range(grids):
+                    source = (row * cols + col) * grids + grid
+                    to_row = (2 * (row // 2) + grid) ^ step
+                    to_col = 2 * (col % 2) + row % 2
+                    target = (to_row * cols + to_col) * grids + col // 2
+                    pairs.append((target, source) if back else (source, target))
+        routes.append(pairs)
+    return routes
+
+
+def cell_norm(values, gain, bias):
+    centre = jnp.mean(values, axis=1, keepdims=True)
+    spread = lax.rsqrt(jnp.mean(values * values, axis=1, keepdims=True) - centre * centre + epsilon)
+    normal = (values - centre) * spread
+    return ((normal * gain + bias).astype(jnp.bfloat16), normal, spread)
+
+
+def cell_norm_back(grad, normal, spread, gain):
+    scaled = grad * gain
+    first = jnp.mean(scaled, axis=1, keepdims=True)
+    second = jnp.mean(scaled * normal, axis=1, keepdims=True)
+    back = (scaled - first - normal * second) * spread
+    return (back, jnp.sum(grad * normal, axis=0), jnp.sum(grad, axis=0))
+
+
+def rotate(values, cosines, sines):
+    half = values.shape[1] // 2
+    low, high = values[:, :half], values[:, half:]
+    return jnp.concatenate([low * cosines - high * sines, high * cosines + low * sines], axis=1)
+
+
+def rotate_back(values, cosines, sines):
+    half = values.shape[1] // 2
+    low, high = values[:, :half], values[:, half:]
+    return jnp.concatenate([low * cosines + high * sines, high * cosines - low * sines], axis=1)
+
+
+def score_cell(query, keys, decay, scale):
+    return (dot(query, keys, 1, 1) * scale * decay).astype(jnp.bfloat16)
+
+
+def mix_cell(query, values, weights, cross, state, scale):
+    scaled = (query.astype(jnp.float32) * (cross * scale)).astype(jnp.bfloat16)
+    return dot(weights, values) + dot(scaled, state.astype(jnp.bfloat16))
+
+
+def value_cell_back(keys, weights, keep, grad_state, grad):
+    kept = (keys.astype(jnp.float32) * keep).astype(jnp.bfloat16)
+    return dot(weights, grad, 0, 0) + dot(kept, grad_state.astype(jnp.bfloat16))
+
+
+def score_cell_back(query, keys, values, decay, cross, keep, state, grad_state, grad, scale):
+    grad_raw = (dot(grad, values, 1, 1) * decay * scale).astype(jnp.bfloat16)
+    grad_added = grad_state.astype(jnp.bfloat16)
+    grad_query = dot(grad_raw, keys) + dot(grad, state.astype(jnp.bfloat16), 1, 1) * (cross * scale)
+    grad_keys = dot(grad_raw, query, 0, 0) + dot(values, grad_added, 1, 1) * keep
+    return (grad_query, grad_keys)
+
+
+def local_cells(
+    tokens,
+    cotangent,
+    lengths,
+    deal_pages,
+    land_slots,
+    pre_gain,
+    pre_bias,
+    query_weight,
+    key_weight,
+    value_weight,
+    gate_weight,
+    group_gain,
+    group_bias,
+    output_weight,
+    mid_gain,
+    mid_bias,
+    up_weight,
+    down_weight,
+):
+    row_index = lax.axis_index("row")
+    col_index = lax.axis_index("col")
+    grid_index = lax.axis_index("grid")
+    col_count = lax.axis_size("col")
+    grid_count = lax.axis_size("grid")
+    batches, tok_dev, half_width = tokens.shape
+    page = tok_dev // 4
+    cell_len = 2 * tok_dev
+    qk_cols = query_weight.shape[1]
+    v_cols = value_weight.shape[1]
+    heads_dev = qk_cols // QK_HEAD
+    scale = QK_HEAD ** (-0.5)
+    everywhere = ("row", "col", "grid")
+
+    places = jnp.stack([row_index, col_index, grid_index])
+    routes, returns = page_routes(False), page_routes(True)
+    half_swap = (row_index + grid_index) % 2
+    page_shape = (batches, page, half_width)
+
+    def join_pages(got):
+        pairs = []
+        for place in range(2):
+            one, two = got[2 * place], got[2 * place + 1]
+            pairs.append(
+                jnp.concatenate(
+                    [jnp.where(half_swap == 0, one, two), jnp.where(half_swap == 0, two, one)], axis=2
+                )
+            )
+        return jnp.concatenate(pairs, axis=1)
+
+    def send_pages(chosen, step):
+        return lax.ppermute(chosen, everywhere, routes[step])
+
+    def deal_pages_of(values):
+        pages = values.reshape(batches, 4, page, half_width)
+        return page_call(deal_kernel, places, deal_pages, [pages], [page_shape] * 4)
+
+    def return_pages(values):
+        got = []
+        for step in range(4):
+            rows = values[:, (step // 2) * page : (step // 2 + 1) * page]
+            first, second = rows[..., :half_width], rows[..., half_width:]
+            sent = jnp.where((half_swap + step) % 2 == 0, first, second)
+            got.append(lax.ppermute(sent, everywhere, returns[step]))
+        pages = page_call(
+            land_kernel, places, deal_pages, got, [(batches, 4, page, half_width)]
+        )[0]
+        return pages.reshape(batches, tok_dev, half_width)
+
+    gains = jnp.stack([pre_gain, pre_bias, mid_gain, mid_bias])
+    gains = jnp.concatenate([gains, swap(gains, "grid", 1)], axis=1)
+    token_pages = deal_pages_of(tokens)
+    local_tokens = join_pages([send_pages(token_pages[step], step) for step in range(4)])
+    pre_gain_all, pre_bias_all, mid_gain_all, mid_bias_all = gains
+
+    own_weights = (
+        jnp.concatenate([query_weight, key_weight], axis=1),
+        value_weight,
+        gate_weight,
+        output_weight,
+        up_weight,
+        down_weight,
+    )
+    own_weights, lengths, land_slots, cotangent = after(
+        (own_weights, lengths, land_slots, cotangent), (gains, tuple(token_pages))
+    )
+    crossed, traded, others = other_halves(own_weights, local_tokens)
+    qk_all, value_all, gate_all, output_all, up_all, down_all = [
+        jnp.concatenate(pair, axis=axis)
+        for *pair, axis in zip(own_weights, others, (0, 0, 0, 1, 0, 1))
+    ]
+
+    head_ids = col_index * heads_dev + jnp.arange(heads_dev, dtype=jnp.int32)
+    log_decay = jnp.log1p(-jnp.exp2(-5.0 - head_ids.astype(jnp.float32)))
+    rates = 10000.0 ** (-jnp.arange(QK_HEAD // 2).astype(jnp.float32) / (QK_HEAD // 2))
+    x_index, core_index = col_index // 2, col_index % 2
+    inner = jnp.arange(page, dtype=jnp.int32)
+    order = jnp.arange(8, dtype=jnp.int32)
+    groups_of = x_index ^ ((order // 2) % 2)
+    sources_of = 2 * ((row_index // 2) ^ (order % 2)) + (core_index ^ (order // 4))
+    slots = land_slots[:, :, row_index, :].reshape(batches, -1)
+    slots = slots[:, (2 * grid_index + groups_of) * 4 + sources_of]
+    positions = (tok_dev * groups_of + page * slots)[:, :, None] + inner
+    positions = positions.reshape(batches, cell_len)
+    runs = lengths[:, row_index, grid_index]
+    slot_order = jnp.arange(runs.shape[1])
+    all_ends = jnp.sum(
+        jnp.where(slot_order[:, None] <= slot_order[None, :], runs[:, :, None], 0), axis=1
+    )
+    tables = []
+    for batch in range(batches):
+        position = positions[batch]
+        angles = position.astype(jnp.float32)[:, None] * rates[None, :]
+        ends = all_ends[batch]
+        segment = jnp.sum((position[:, None] >= ends[None, :]).astype(jnp.int32), axis=1)
+        last = jnp.sum((cell_len - 1 >= ends).astype(jnp.int32))
+        distance = position[:, None] - position[None, :]
+        same = (segment[:, None] == segment[None, :]) & (distance >= 0)
+        span = jnp.maximum(distance, 0).astype(jnp.float32)
+        decays = [
+            jnp.where(same, jnp.exp(log_decay[head] * span), 0.0) for head in range(heads_dev)
+        ]
+        crosses = [
+            jnp.where(
+                segment == -1, jnp.exp(log_decay[head] * (position + 1).astype(jnp.float32)), 0.0
+            )[:, None]
+            for head in range(heads_dev)
+        ]
+        keeps = [
+            jnp.where(
+                segment == last,
+                jnp.exp(log_decay[head] * (cell_len - 1 - position).astype(jnp.float32)),
+                0.0,
+            )[:, None]
+            for head in range(heads_dev)
+        ]
+        tables.append((jnp.cos(angles), jnp.sin(angles), decays, crosses, keeps))
+    state = jnp.zeros((QK_HEAD, V_HEAD), jnp.float32)
+    grad_state = jnp.zeros((QK_HEAD, V_HEAD), jnp.float32)
+
+    marks = [()]
+
+    def hold(values, *others):
+        return after(values, (marks[0], *others))
+
+    def mark(*values):
+        marks[0] = values
+
+    def tall(parts):
+        return jnp.concatenate(parts, axis=0)
+
+    every = range(batches)
+    head_slices = [slice(head * V_HEAD, (head + 1) * V_HEAD) for head in range(heads_dev)]
+    inputs, normal_one, cell_one = [], [], []
+    for batch in every:
+        inputs.append(hold(local_tokens[batch], crossed[0]).astype(jnp.float32))
+        hidden, unit, spread = cell_norm(inputs[batch], pre_gain_all, pre_bias_all)
+        normal_one.append((unit, spread))
+        mark(hidden)
+        cell_one.append(gather_cell(hidden))
+
+    scores, heads, grads_got = [], [], []
+    grad_pages = list(hold(tuple(deal_pages_of(cotangent))))
+    for batch in every:
+        cosines, sines, decays, crosses, keeps = tables[batch]
+        qk_raw = dot(hold(cell_one[batch], *crossed[1 : 1 + batch]), qk_all)
+        parts = []
+        for head in range(heads_dev):
+            qk = slice(head * QK_HEAD, (head + 1) * QK_HEAD)
+            query = rotate(qk_raw[:, qk], cosines, sines).astype(jnp.bfloat16)
+            keys = rotate(qk_raw[:, qk_cols:][:, qk], cosines, sines).astype(jnp.bfloat16)
+            parts.append((query, keys, score_cell(query, keys, decays[head], scale)))
+        scores.append(parts)
+        mark([part[2] for part in parts])
+        pair = hold(tuple(grad_pages[2 * batch : 2 * batch + 2]))
+        grads_got.extend(send_pages(pair[place], 2 * batch + place) for place in range(2))
+    for batch in every:
+        crosses = tables[batch][3]
+        value_low = dot(hold(cell_one[batch], *crossed[2 : 2 + batch]), value_all).astype(jnp.bfloat16)
+        kept = []
+        for head, vs in enumerate(head_slices):
+            query, keys, weights = scores[batch][head]
+            values = value_low[:, vs]
+            mixed = mix_cell(query, values, weights, crosses[head], state, scale)
+            centred = mixed - jnp.mean(mixed, axis=1, keepdims=True)
+            spread = lax.rsqrt(jnp.mean(centred * centred, axis=1, keepdims=True) + epsilon)
+            kept.append((query, keys, values, weights, centred * spread, spread))
+        heads.append(kept)
+        mark([one[4] for one in kept])
+    local_grads = hold(join_pages(grads_got))
+    top_cells = gather_cell(local_grads, axis=1)
+    top_cell = [top_cells[batch] for batch in every]
+    top_tall = top_cells.reshape(-1, top_cells.shape[2])
+    gates, unit_out = [], []
+    for batch in every:
+        gate = dot(hold(cell_one[batch], *crossed[3 : 3 + batch]), gate_all)
+        gated = []
+        for head, vs in enumerate(head_slices):
+            scaled = heads[batch][head][4] * group_gain[vs] + group_bias[vs]
+            gated.append((gate[:, vs] * jax.nn.sigmoid(gate[:, vs]) * scaled).astype(jnp.bfloat16))
+        gates.append([gate[:, vs] for vs in head_slices])
+        unit_out.append(jnp.concatenate(gated, axis=1))
+        mark(unit_out[batch])
+    attn_out = []
+    for batch in every:
+        part = dot(hold(unit_out[batch], *crossed[4 : 4 + batch]), output_all).astype(jnp.bfloat16)
+        mark(part)
+        attn_out.append(scatter_cell(part))
+
+    resid, normal_two, cell_two = [], [], []
+    for batch in every:
+        resid.append(inputs[batch] + hold(attn_out[batch], crossed[5]))
+        hidden, unit, spread = cell_norm(resid[batch], mid_gain_all, mid_bias_all)
+        normal_two.append((unit, spread))
+        mark(hidden)
+        cell_two.append(gather_cell(hidden))
+
+    activated, grad_pre, grad_two = [], [], []
+    for batch in every:
+        pre_act = dot(hold(cell_two[batch]), up_all)
+        active, gelu_pull = jax.vjp(exact_gelu, pre_act)
+        activated.append(active.astype(jnp.bfloat16))
+        (grad,) = gelu_pull(dot(top_cell[batch], down_all, 1, 1))
+        grad_pre.append(grad.astype(jnp.bfloat16))
+        part = dot(grad_pre[batch], up_all, 1, 1).astype(jnp.bfloat16)
+        mark(part, activated[batch])
+        grad_two.append(scatter_cell(part))
+
+    row_edge = (row_index == 0) | (row_index == 3)
+    chunks, swapped, fresh_sums, row_sums, totals, finals = [], [], {}, {}, {}, []
+    flights = []
+
+    def chunk_dots(left, right, axis):
+        made = []
+        for place in range(2):
+            rows = slice(place * 512, place * 512 + 512)
+            if axis == 1:
+                own, other = (left[:, rows], right[:, :1024]), (left[:, rows], right[:, 1024:])
+            else:
+                own = (left[:, rows], right)
+                other = (left[:, 1024 + place * 512 : 1024 + place * 512 + 512], right)
+            made.append((dot(*own, 0, 0), dot(*other, 0, 0).astype(jnp.bfloat16)))
+        mark(made)
+        return made
+
+    def tick(chunk=None):
+        now = len(flights)
+        past = flights[-1] if flights else ()
+        flying = []
+        first, second, third = now - 1, now - 2, now - 3
+        fresh = total = None
+        if 0 <= first < len(chunks):
+            fresh = (chunks[first] + swapped[first].astype(jnp.float32)).astype(jnp.bfloat16)
+        if 0 <= third < len(chunks):
+            total = totals[third]
+        if chunk is not None:
+            own, other = chunk
+            swapped.append(swap(after(other, past), "grid", 1))
+            chunks.append(own)
+            flying.append(swapped[now])
+        if 0 <= second < len(row_sums):
+            other = lax.ppermute(after(row_sums[second], past), "row", [(1, 2), (2, 1)])
+            flying.append(other)
+            totals[second] = (
+                row_sums[second].astype(jnp.float32) + other.astype(jnp.float32)
+            ).astype(jnp.bfloat16)
+        if fresh is not None or total is not None:
+            if total is None:
+                sent, pairs = fresh, [(0, 1), (3, 2)]
+            elif fresh is None:
+                sent, pairs = total, [(1, 0), (2, 3)]
+            else:
+                sent = jnp.where(row_edge, fresh, total)
+                pairs = [(0, 1), (1, 0), (2, 3), (3, 2)]
+            got = lax.ppermute(after(sent, past), "row", pairs)
+            flying.append(got)
+            if fresh is not None:
+                row_sums[first] = (fresh.astype(jnp.float32) + got.astype(jnp.float32)).astype(
+                    jnp.bfloat16
+                )
+            if total is not None:
+                finals.append(jnp.where(row_edge, got, total).astype(jnp.float32))
+        marks[0] = (marks[0], past)
+        flights.append(tuple(flying))
+
+    down_chunks = chunk_dots(hold(tall(activated)), top_tall, 1)
+    tick(down_chunks[0])
+    down_out = jnp.stack([dot(hold(one), down_all).astype(jnp.bfloat16) for one in activated])
+    mark(down_out)
+    ffn_out = scatter_cell(down_out, axis=1)
+
+    grad_resid, mid_cell, mid_parts = [], [], []
+    for batch in every:
+        unit, spread = normal_two[batch]
+        back, *small = cell_norm_back(hold(grad_two[batch]), unit, spread, mid_gain_all)
+        mid_parts.append(small)
+        grad_resid.append(local_grads[batch].astype(jnp.float32) + back)
+        low = grad_resid[batch].astype(jnp.bfloat16)
+        mark(low)
+        mid_cell.append(gather_cell(low))
+        if batch == 0:
+            tick(down_chunks[1])
+    up_chunks = chunk_dots(hold(tall(cell_two)), tall(grad_pre), 0)
+    tick(up_chunks[0])
+    results = (jnp.stack(resid) + hold(ffn_out)).astype(jnp.bfloat16)
+    mark(results)
+    block_out = return_pages(results)
+
+    grad_mixed, grad_gate, grad_value, group_parts = [], [], [], []
+    for batch in every:
+        keeps = tables[batch][4]
+        grad_unit = dot(hold(mid_cell[batch]), output_all, 1, 1)
+        mixed_parts, gate_parts, value_parts, gain_parts, bias_parts = [], [], [], [], []
+        for head, vs in enumerate(head_slices):
+            query, keys, values, weights, normal, spread = heads[batch][head]
+            gate_part = gates[batch][head]
+            grad_u = grad_unit[:, vs]
+            sig = jax.nn.sigmoid(gate_part)
+            scaled = normal * group_gain[vs] + group_bias[vs]
+            gate_parts.append(
+                (grad_u * scaled * (sig * (1.0 + gate_part * (1.0 - sig)))).astype(jnp.bfloat16)
+            )
+            grad_scaled = grad_u * (gate_part * sig)
+            gain_parts.append(jnp.sum(grad_scaled * normal, axis=0))
+            bias_parts.append(jnp.sum(grad_scaled, axis=0))
+            grad_normal = grad_scaled * group_gain[vs]
+            grad = spread * (
+                grad_normal
+                - jnp.mean(grad_normal, axis=1, keepdims=True)
+                - normal * jnp.mean(grad_normal * normal, axis=1, keepdims=True)
+            )
+            mixed_parts.append(grad.astype(jnp.bfloat16))
+            value_parts.append(
+                value_cell_back(keys, weights, keeps[head], grad_state, mixed_parts[head]).astype(
+                    jnp.bfloat16
+                )
+            )
+        grad_mixed.append(mixed_parts)
+        grad_gate.append(jnp.concatenate(gate_parts, axis=1))
+        grad_value.append(jnp.concatenate(value_parts, axis=1))
+        group_parts.append((jnp.concatenate(gain_parts), jnp.concatenate(bias_parts)))
+        mark(grad_gate[batch], grad_value[batch])
+        if batch == 0:
+            tick(up_chunks[1])
+    out_chunks = chunk_dots(hold(tall(unit_out), block_out), tall(mid_cell), 1)
+    tick(out_chunks[0])
+    cells = tall(cell_one)
+    gate_chunks = chunk_dots(hold(cells), tall(grad_gate), 0)
+    tick(out_chunks[1])
+    grad_qk = []
+    for batch in every:
+        cosines, sines, decays, crosses, keeps = tables[batch]
+        query_parts, key_parts = [], []
+        for head in range(heads_dev):
+            query, keys, values, weights, normal, spread = heads[batch][head]
+            grad_query, grad_keys = score_cell_back(
+                query,
+                keys,
+                values,
+                decays[head],
+                crosses[head],
+                keeps[head],
+                state,
+                grad_state,
+                hold(grad_mixed[batch][head]),
+                scale,
+            )
+            query_parts.append(rotate_back(grad_query, cosines, sines).astype(jnp.bfloat16))
+            key_parts.append(rotate_back(grad_keys, cosines, sines).astype(jnp.bfloat16))
+        grad_qk.append(jnp.concatenate(query_parts + key_parts, axis=1))
+        mark(grad_qk[batch])
+        tick(gate_chunks[batch])
+    value_chunks = chunk_dots(hold(cells), tall(grad_value), 0)
+    tick(value_chunks[0])
+    qk_chunks = chunk_dots(hold(cells), tall(grad_qk), 0)
+    tick(value_chunks[1])
+
+    grad_one = []
+    for batch in every:
+        part = (
+            dot(hold(grad_qk[batch]), qk_all, 1, 1)
+            + dot(grad_value[batch], value_all, 1, 1)
+            + dot(grad_gate[batch], gate_all, 1, 1)
+        ).astype(jnp.bfloat16)
+        mark(part)
+        grad_one.append(scatter_cell(part))
+        tick(qk_chunks[batch])
+    pre_parts, input_grads = [], []
+    for batch in every:
+        unit, spread = normal_one[batch]
+        back, *small = cell_norm_back(hold(grad_one[batch]), unit, spread, pre_gain_all)
+        pre_parts.append(small)
+        input_grads.append((grad_resid[batch] + back).astype(jnp.bfloat16))
+        mark(input_grads[batch])
+    tokens_grad = return_pages(jnp.stack(input_grads))
+    for _ in range(3):
+        tick()
+    down_grad, up_grad, out_grad, gating_grad, value_grad = [
+        jnp.concatenate(finals[place : place + 2], axis=0) for place in range(0, 10, 2)
+    ]
+    query_grad = jnp.concatenate([part[:, :qk_cols] for part in finals[10:]], axis=0)
+    key_grad = jnp.concatenate([part[:, qk_cols:] for part in finals[10:]], axis=0)
+
+    feature_len = pre_gain.shape[0]
+    features = jnp.stack([sum(parts) for parts in (*zip(*pre_parts), *zip(*mid_parts))])
+    groups = jnp.stack([sum(parts) for parts in zip(*group_parts)])
+    sent = jnp.concatenate([features[:, feature_len:], groups])
+    smalls = jnp.concatenate([features[:, :feature_len], groups]) + swap(sent, "grid", 1)
+    smalls = smalls + swap(smalls, "row", 1)
+    smalls = smalls + swap(smalls, "row", 2)
+    features, groups = smalls[:4], smalls[4:]
+    features = features + swap(features, "col", 1)
+    features = features + swap(features, "col", 2)
+    return (
+        block_out,
+        tokens_grad,
+        features[0],
+        features[1],
+        query_grad,
+        key_grad,
+        value_grad,
+        gating_grad,
+        groups[0],
+        groups[1],
+        out_grad,
+        features[2],
+        features[3],
+        up_grad,
+        down_grad,
+    )
+
+
+def local(*arguments):
+    tokens, query_weight = arguments[0], arguments[7]
+    sizes = tuple(lax.axis_size(axis) for axis in ("row", "col", "grid"))
+    one_block = 2 * tokens.shape[1] == CH
+    if sizes == (4, 4, 2) and one_block and query_weight.shape[1] % QK_HEAD == 0:
+        return local_cells(*arguments)
+    return local_general(*arguments)
+
+
 def solution(mesh):
     placed = (
         P(None, ("row", "col"), "grid"),

time: 2380 us -> 915 us (0.38)
  waiting for transfers between devices: 1900 us -> 377 us
  starting transfers between devices: 20.5 us -> 135 us
  local copies, waits for them, and re-layouts: 107 us -> 42.1 us
  matrix products: 187 us -> 233 us
    reduce_scatter x16 -> x0, waiting for transfers between devices: 891 us -> none  [the longest x4 375 us: project_in(): lax.psum_scatter(term(jnp.int32(0), lax.axis_size('grid') * rows), 'grid'...]
    psum x2 -> x0, waiting for transfers between devices: 500 us -> none  [the longest x1 421 us: sum_rows(): lax.psum(shortened(grads), 'row')]
    all_gather x16 -> x0, waiting for transfers between devices: 438 us -> none  [the longest x4 189 us: back_in(): grad_all = lax.all_gather(grad, 'grid', axis=0, tiled=True)]
    ppermute x0 -> x100, waiting for transfers between devices: none -> 377 us  [the longest x52 177 us: swap(): lax.ppermute(values, axis, [(one, one ^ bit) for one in range(count)])]
    ppermute x0 -> x100, starting transfers between devices: none -> 135 us  [the longest x52 47 us: swap(): lax.ppermute(values, axis, [(one, one ^ bit) for one in range(count)])]
    all_to_all x4 -> x0, waiting for transfers between devices: 70.8 us -> none  [the longest x1 24.7 us: local(): lax.all_to_all(pick(paged(tokens), send_order), 'row', split_axis=1, conc...]
    dot_general x44 -> x88, matrix products: 187 us -> 233 us  [dot(): lax.dot_general(left, right, (((left_axis,), (right_axis,)), ((), ())), p...]
    convert_element_type x20 -> x24, other arithmetic: 55.4 us -> 14.7 us  [the longest x12 8.71 us: tick(): (fresh.astype(jnp.float32) + got.astype(jnp.float32)).astype(jnp.bfloat16)]
  transfers between devices with their start and end apart: 38 -> 100, of which waited for: 37 -> 38; matrix products, arithmetic and copies ran while one was open for 11% -> 39% of each run, Pallas kernels for 0% -> 1%
where the time goes in v2:
time: 915 us; the launch traced here: 906 us
  waiting for transfers between devices  377 us (41%)
  matrix products  233 us (25%)
  starting transfers between devices  135 us (15%)
  other arithmetic  106 us (12%)
  local copies, waits for them, and re-layouts  42.1 us (5%)
    dot_general x88, matrix products, dot(): lax.dot_general(left, right, (((left_axis,), (right_axis,)), ((), ())), p...  233 us
    ppermute x52, waiting for transfers between devices, swap(): lax.ppermute(values, axis, [(one, one ^ bit) for one in range(count)])  177 us
    ppermute x14, waiting for transfers between devices, tick(): got = lax.ppermute(after(sent, past), 'row', pairs)  122 us
    ppermute x6, waiting for transfers between devices, other_halves(): traded.append(lax.ppermute(crossed[place], 'row', pairs))  47.1 us
    ppermute x52, starting transfers between devices, swap(): lax.ppermute(values, axis, [(one, one ^ bit) for one in range(count)])  47 us
    ppermute x14, starting transfers between devices, tick(): got = lax.ppermute(after(sent, past), 'row', pairs)  37.2 us
    unnamed x401, local copies, waits for them, and re-layouts  26.7 us
    unnamed x20, other arithmetic  22.8 us
  transfers between devices with their start and end apart: 100, of which 38 were waited for; matrix products, arithmetic and copies ran while one was open for 39% of the time, Pallas kernels for 1%

profile of v2, /device:TPU:0, one launch (start us, length us, event | category | flops | bytes accessed | tf_op | source)
XLA Modules:
  0.0 906.2 jit_solution(4135918782094299334)
XLA Ops:
  35.8 17.4 %collective-permute-done.5 = bf16[512,1024]{1,0:T(8,128)(2,1)} collective-permute-done((bf16[512,1024]{1,0:T(8,128)(2,1)}, bf16[512,1024]{1,0:T(8,128)(2,1)}, u32[]{:S(2)}, u32[]{:S(2)}) %collective-permute-start.5) | collective-permute-done | bytes 1048608 | tf_op jit(solution)/shard_map/ppermute | solution.py:480
  72.7 11.2 %collective-permute-done.11 = bf16[512,1024]{1,0:T(8,128)(2,1)} collective-permute-done((bf16[512,1024]{1,0:T(8,128)(2,1)}, bf16[512,1024]{1,0:T(8,128)(2,1)}, u32[]{:S(2)}, u32[]{:S(2)}) %collective-permute-start.11) | collective-permute-done | bytes 1048608 | tf_op jit(solution)/shard_map/ppermute | solution.py:480
  106.6 6.2 collective-permute-done.29
  142.5 9.3 %collective-permute-done.14 = bf16[512,1024]{1,0:T(8,128)(2,1)S(1)} collective-permute-done((bf16[512,1024]{1,0:T(8,128)(2,1)S(1)}, bf16[512,1024]{1,0:T(8,128)(2,1)S(1)}, u32[]{:S(2)}, u32[]{:S(2)}) %collective-permute-start.14) | collective-permute-done | bytes 1048608 | tf_op jit(solution)/shard_map/ppermute | solution.py:509
  164.7 18.4 %collective-permute-done.16 = bf16[512,1024]{1,0:T(8,128)(2,1)S(1)} collective-permute-done((bf16[512,1024]{1,0:T(8,128)(2,1)S(1)}, bf16[512,1024]{1,0:T(8,128)(2,1)S(1)}, u32[]{:S(2)}, u32[]{:S(2)}) %collective-permute-start.16) | collective-permute-done | bytes 1048608 | tf_op jit(solution)/shard_map/ppermute | solution.py:509
  183.2 9.5 %convolution_convert_fusion.5 = bf16[512,2048]{1,0:T(8,128)(2,1)S(1)} fusion(bf16[512,1024]{0,1:T(8,128)(2,1)S(1)} %pad_maximum_fusion.20, bf16[512,1024]{1,0:T(8,128)(2,1)S(1)} %get-tuple-element.338, bf16[512,1024]{1,0:T(8,128)(2,1)S(1)} %get-tuple-element.337, bf16[1024,1024]{1,0:T(8,128)(2,1)S(1)} %copy-done.111), kind=kOutput, calls=%fused_computation.22 | convolution fusion | flops 2161115136 | bytes 7340032 | tf_op jit(solution)/shard_map/dot_general | solution.py:517
  194.2 9.6 %convolution_convert_fusion.4 = bf16[512,2048]{1,0:T(8,128)(2,1)S(1)} fusion(bf16[512,1024]{0,1:T(8,128)(2,1)S(1)} %pad_maximum_fusion.21, bf16[512,1024]{1,0:T(8,128)(2,1)S(1)} %get-tuple-element.338, bf16[512,1024]{1,0:T(8,128)(2,1)S(1)} %get-tuple-element.337, bf16[1024,1024]{1,0:T(8,128)(2,1)S(1)} %copy-done.111), kind=kOutput, calls=%fused_computation.21 | convolution fusion | flops 2161115136 | bytes 7340032 | tf_op jit(solution)/shard_map/dot_general | solution.py:517
  209.2 9.3 %collective-permute-done.20 = bf16[512,1024]{1,0:T(8,128)(2,1)S(1)} collective-permute-done((bf16[512,1024]{1,0:T(8,128)(2,1)S(1)}, bf16[512,1024]{1,0:T(8,128)(2,1)S(1)}, u32[]{:S(2)}, u32[]{:S(2)}) %collective-permute-start.20) | collective-permute-done | bytes 1048608 | tf_op jit(solution)/shard_map/ppermute | solution.py:480
  218.8 11.4 %collective-permute-done.25 = bf16[512,1024]{1,0:T(8,128)(2,1)S(1)} collective-permute-done((bf16[512,1024]{1,0:T(8,128)(2,1)S(1)}, bf16[512,1024]{1,0:T(8,128)(2,1)S(1)}, u32[]{:S(2)}, u32[]{:S(2)}) %collective-permute-start.25) | collective-permute-done | bytes 1048608 | tf_op jit(solution)/shard_map/ppermute | solution.py:509
  232.3 11.5 %collective-permute-done.23 = bf16[128,2048]{1,0:T(8,128)(2,1)S(1)} collective-permute-done((bf16[128,2048]{1,0:T(8,128)(2,1)S(1)}, bf16[128,2048]{1,0:T(8,128)(2,1)S(1)}, u32[]{:S(2)}, u32[]{:S(2)}) %collective-permute-start.23) | collective-permute-done | bytes 524320 | tf_op jit(solution)/shard_map/ppermute | solution.py:480
  244.0 8.0 collective-permute-done.34
  258.0 12.9 %multiply_convert_fusion.1 = (bf16[512,1024]{1,0:T(8,128)(2,1)S(1)}, f32[512,1024]{1,0:T(8,128)S(1)}, f32[512,1024]{1,0:T(8,128)}) fusion(bf16[512,2048]{1,0:T(8,128)(2,1)S(1)} %pad_maximum_fusion.8, bf16[512,1024]{1,0:T(8,128)(2,1)S(1)} %get-tuple-element.336, bf16[512,1024]{1,0:T(8,128)(2,1)S(1)} %get-tuple-element.335, ...), kind=kOutput, calls=%fused_computation.113 | convolution fusion | flops 2194145280 | bytes 11534336 | tf_op jit(solution)/shard_map/dot_general | solution.py:517
  270.9 12.4 %add_convert_fusion.39 = bf16[512,1024]{1,0:T(8,128)(2,1)S(1)} fusion(f32[512,1024]{1,0:T(8,128)S(1)} %get-tuple-element.290, f32[512,1024]{1,0:T(8,128)} %get-tuple-element.416, bf16[2,512,2048]{2,1,0:T(8,128)(2,1)} %copy-done.126, bf16[512,1024]{1,0:T(8,128)(2,1)S(1)} %get-tuple-element.334, bf16[512,1024]{1,0:T(8,128)(2,1)S(1)} %get-tuple-element.333, ...), kind=kOutput, calls=%fused_computation.112 | convolution fusion | flops 2167406592 | bytes 11534336 | tf_op jit(solution)/shard_map/dot_general | solution.py:517
  283.3 5.7 convolution_convert_fusion.3
  297.5 7.9 multiply_convert_fusion
  305.4 6.7 add_convert_fusion.38
  312.1 5.8 convolution_convert_fusion.2
  326.8 12.1 %collective-permute-done.48 = bf16[128,2048]{1,0:T(8,128)(2,1)S(1)} collective-permute-done((bf16[128,2048]{1,0:T(8,128)(2,1)S(1)}, bf16[128,2048]{1,0:T(8,128)(2,1)S(1)}, u32[]{:S(2)}, u32[]{:S(2)}) %collective-permute-start.48) | collective-permute-done | bytes 524320 | tf_op jit(solution)/shard_map/ppermute | solution.py:480
  340.4 6.3 collective-permute-done.41
  361.6 9.5 %collective-permute-done.42 = bf16[512,1024]{1,0:T(8,128)(2,1)} collective-permute-done((bf16[512,1024]{1,0:T(8,128)(2,1)S(1)}, bf16[512,1024]{1,0:T(8,128)(2,1)}, u32[]{:S(2)}, u32[]{:S(2)}) %collective-permute-start.42) | collective-permute-done | bytes 1048608 | tf_op jit(solution)/shard_map/ppermute | solution.py:480
  380.5 9.6 %fusion = bf16[1,512,2048]{2,1,0:T(8,128)(2,1)S(1)} fusion(bf16[512,1024]{1,0:T(8,128)(2,1)S(1)} %get-tuple-element.164, bf16[512,1024]{1,0:T(8,128)(2,1)S(1)} %get-tuple-element.334, bf16[512,1024]{1,0:T(8,128)(2,1)S(1)} %get-tuple-element.333, bf16[1024,1024]{1,0:T(8,128)(2,1)S(1)} %copy-done.109), kind=kOutput, calls=%fused_computation.23 | convolution fusion | flops 2161115136 | bytes 7340032 | tf_op jit(solution)/shard_map/dot_general | solution.py:517
  391.4 9.2 %fusion.1 = bf16[1,512,2048]{2,1,0:T(8,128)(2,1)S(1)} fusion(bf16[512,1024]{1,0:T(8,128)(2,1)S(1)} %copy-done.81, bf16[512,1024]{1,0:T(8,128)(2,1)S(1)} %get-tuple-element.334, bf16[512,1024]{1,0:T(8,128)(2,1)S(1)} %get-tuple-element.333, bf16[1024,1024]{1,0:T(8,128)(2,1)S(1)} %copy-done.109), kind=kOutput, calls=%fused_computation.24 | convolution fusion | flops 2161115136 | bytes 7340032 | tf_op jit(solution)/shard_map/dot_general | solution.py:517
  421.6 15.5 %collective-permute-done.57 = bf16[512,1024]{1,0:T(8,128)(2,1)S(1)} collective-permute-done((bf16[512,1024]{1,0:T(8,128)(2,1)S(1)}, bf16[512,1024]{1,0:T(8,128)(2,1)S(1)}, u32[]{:S(2)}, u32[]{:S(2)}) %collective-permute-start.57) | collective-permute-done | bytes 1048608 | tf_op jit(solution)/shard_map/ppermute | solution.py:890
  466.0 17.7 %collective-permute-done.46.refs_2_ = bf16[2,64,1024]{2,1,0:T(8,128)(2,1)S(1)} collective-permute-done((bf16[2,64,1024]{2,1,0:T(8,128)(2,1)S(1)}, bf16[2,64,1024]{2,1,0:T(8,128)(2,1)S(1)}, u32[]{:S(2)}, u32[]{:S(2)}) %collective-permute-start.46) | collective-permute-done | bytes 262176 | tf_op jit(solution)/shard_map/ppermute | solution.py:679
  495.6 7.0 collective-permute-done.60
  504.4 12.8 %collective-permute-done.58 = bf16[512,1024]{1,0:T(8,128)(2,1)S(1)} collective-permute-done((bf16[512,1024]{1,0:T(8,128)(2,1)S(1)}, bf16[512,1024]{1,0:T(8,128)(2,1)S(1)}, u32[]{:S(2)}, u32[]{:S(2)}) %collective-permute-start.58) | collective-permute-done | bytes 1048608 | tf_op jit(solution)/shard_map/ppermute | solution.py:480
  525.6 7.1 fusion.409
  532.7 13.5 %collective-permute-done.63 = bf16[512,1024]{1,0:T(8,128)(2,1)S(1)} collective-permute-done((bf16[512,1024]{1,0:T(8,128)(2,1)S(1)}, bf16[512,1024]{1,0:T(8,128)(2,1)S(1)}, u32[]{:S(2)}, u32[]{:S(2)}) %collective-permute-start.63) | collective-permute-done | bytes 1048608 | tf_op jit(solution)/shard_map/ppermute | solution.py:890
  550.1 6.6 collective-permute-start.66
  560.4 19.0 %collective-permute-done.66 = bf16[512,1024]{1,0:T(8,128)(2,1)S(1)} collective-permute-done((bf16[512,1024]{1,0:T(8,128)(2,1)S(1)}, bf16[512,1024]{1,0:T(8,128)(2,1)S(1)}, u32[]{:S(2)}, u32[]{:S(2)}) %collective-permute-start.66) | collective-permute-done | bytes 1048608 | tf_op jit(solution)/shard_map/ppermute | solution.py:890
  583.8 7.2 fusion.407
  595.6 10.8 %collective-permute-done.67 = bf16[512,1024]{1,0:T(8,128)(2,1)S(1)} collective-permute-done((bf16[512,1024]{1,0:T(8,128)(2,1)S(1)}, bf16[512,1024]{1,0:T(8,128)(2,1)S(1)}, u32[]{:S(2)}, u32[]{:S(2)}) %collective-permute-start.67) | collective-permute-done | bytes 1048608 | tf_op jit(solution)/shard_map/ppermute | solution.py:480
  654.9 11.7 %collective-permute-done.70 = bf16[512,1024]{1,0:T(8,128)(2,1)S(1)} collective-permute-done((bf16[512,1024]{1,0:T(8,128)(2,1)S(1)}, bf16[512,1024]{1,0:T(8,128)(2,1)S(1)}, u32[]{:S(2)}, u32[]{:S(2)}) %collective-permute-start.70) | collective-permute-done | bytes 1048608 | tf_op jit(solution)/shard_map/ppermute | solution.py:480
  668.0 6.8 collective-permute-done.72
  684.6 11.9 %collective-permute-done.77 = bf16[512,1024]{1,0:T(8,128)(2,1)S(1)} collective-permute-done((bf16[512,1024]{1,0:T(8,128)(2,1)S(1)}, bf16[512,1024]{1,0:T(8,128)(2,1)S(1)}, u32[]{:S(2)}, u32[]{:S(2)}) %collective-permute-start.77) | collective-permute-done | bytes 1048608 | tf_op jit(solution)/shard_map/ppermute | solution.py:890
  699.3 6.0 collective-permute-start.80
  711.2 10.1 %collective-permute-done.80 = bf16[512,1024]{1,0:T(8,128)(2,1)S(1)} collective-permute-done((bf16[512,1024]{1,0:T(8,128)(2,1)S(1)}, bf16[512,1024]{1,0:T(8,128)(2,1)S(1)}, u32[]{:S(2)}, u32[]{:S(2)}) %collective-permute-start.80) | collective-permute-done | bytes 1048608 | tf_op jit(solution)/shard_map/ppermute | solution.py:890
  721.9 6.8 collective-permute-done.78
  740.1 6.5 collective-permute-done.93
  750.7 8.2 fusion.418
  758.9 6.8 add_convert_fusion.1
  765.7 8.2 fusion.417
  774.0 6.8 add_convert_fusion
  790.6 20.3 %collective-permute-done.96 = bf16[512,1024]{1,0:T(8,128)(2,1)S(1)} collective-permute-done((bf16[512,1024]{1,0:T(8,128)(2,1)S(1)}, bf16[512,1024]{1,0:T(8,128)(2,1)S(1)}, u32[]{:S(2)}, u32[]{:S(2)}) %collective-permute-start.96) | collective-permute-done | bytes 1048608 | tf_op jit(solution)/shard_map/ppermute | solution.py:890
  825.0 6.2 collective-permute-start.88
  831.9 11.3 %collective-permute-done.88 = f32[6,1024]{1,0:T(8,128)S(1)} collective-permute-done((f32[6,1024]{1,0:T(8,128)S(1)}, f32[6,1024]{1,0:T(8,128)S(1)}, u32[]{:S(2)}, u32[]{:S(2)}) %collective-permute-start.88) | collective-permute-done | bytes 24608 | tf_op jit(solution)/shard_map/ppermute | solution.py:480
  857.1 20.1 %collective-permute-done.91 = f32[4,1024]{1,0:T(4,128)S(1)} collective-permute-done((f32[4,1024]{1,0:T(4,128)S(1)}, f32[4,1024]{1,0:T(4,128)S(1)}, u32[]{:S(2)}, u32[]{:S(2)}) %collective-permute-start.91) | collective-permute-done | bytes 16416 | tf_op jit(solution)/shard_map/ppermute | solution.py:480
  883.8 17.7 %collective-permute-done.99 = bf16[512,1024]{1,0:T(8,128)(2,1)} collective-permute-done((bf16[512,1024]{1,0:T(8,128)(2,1)S(1)}, bf16[512,1024]{1,0:T(8,128)(2,1)}, u32[]{:S(2)}, u32[]{:S(2)}) %collective-permute-start.99) | collective-permute-done | bytes 1048608 | tf_op jit(solution)/shard_map/ppermute | solution.py:890
  (875 shorter events, 398.4 us)
Async XLA Ops:
  10.0 25.4 %collective-permute-start.3 = (bf16[2,64,1024]{2,1,0:T(8,128)(2,1)}, bf16[2,64,1024]{2,1,0:T(8,128)(2,1)S(1)}, u32[]{:S(2)}, u32[]{:S(2)}) collective-permute-start(bf16[2,64,1024]{2,1,0:T(8,128)(2,1)} %get-tuple-element.121), channel_id=1, source_target_pairs={{0,24},{1,16},{2,28},{3,20},{4,25},{5,17},{6,29},{7,21},{8,26},{9,... | collective-permute-start | bytes 786440 | tf_op jit(solution)/shard_map/ppermute | solution.py:667
  22.6 30.6 %collective-permute-start.5 = (bf16[512,1024]{1,0:T(8,128)(2,1)}, bf16[512,1024]{1,0:T(8,128)(2,1)}, u32[]{:S(2)}, u32[]{:S(2)}) collective-permute-start(bf16[512,1024]{1,0:T(8,128)(2,1)} %constant_dynamic-slice_fusion.7), channel_id=1, source_target_pairs={{0,1},{1,0},{2,3},{3,2},{4,5},{5,4},{6,7},{7,6},{8,9},{9,8},{10,11... | collective-permute-start | bytes 3145736 | tf_op jit(solution)/shard_map/ppermute | solution.py:480
  58.9 24.9 %collective-permute-start.11 = (bf16[512,1024]{1,0:T(8,128)(2,1)}, bf16[512,1024]{1,0:T(8,128)(2,1)}, u32[]{:S(2)}, u32[]{:S(2)}) collective-permute-start(bf16[512,1024]{1,0:T(8,128)(2,1)} %constant_dynamic-slice_fusion.4), channel_id=1, source_target_pairs={{0,1},{1,0},{2,3},{3,2},{4,5},{5,4},{6,7},{7,6},{8,9},{9,8},{10,11... | collective-permute-start | bytes 3145736 | tf_op jit(solution)/shard_map/ppermute | solution.py:480
  59.0 26.9 %collective-permute-start.10 = (bf16[512,1024]{1,0:T(8,128)(2,1)}, bf16[512,1024]{1,0:T(8,128)(2,1)}, u32[]{:S(2)}, u32[]{:S(2)}) collective-permute-start(bf16[512,1024]{1,0:T(8,128)(2,1)} %collective-permute-done.5), channel_id=1, source_target_pairs={{0,8},{8,0},{16,24},{24,16},{1,9},{9,1},{17,25},{25,17},{2,10},{10... | collective-permute-start | bytes 3145736 | tf_op jit(solution)/shard_map/ppermute | solution.py:509
  83.9 29.9 %collective-permute-start.13 = (bf16[512,1024]{1,0:T(8,128)(2,1)S(1)}, bf16[512,1024]{1,0:T(8,128)(2,1)S(1)}, u32[]{:S(2)}, u32[]{:S(2)}) collective-permute-start(bf16[512,1024]{1,0:T(8,128)(2,1)S(1)} %copy-done.79), channel_id=1, source_target_pairs={{0,1},{1,0},{2,3},{3,2},{4,5},{5,4},{6,7},{7,6},{8,9},{9,8},{10,11... | collective-permute-start | bytes 3145736 | tf_op jit(solution)/shard_map/ppermute | solution.py:480
  84.1 34.5 %collective-permute-start.12 = (bf16[512,1024]{1,0:T(8,128)(2,1)}, bf16[512,1024]{1,0:T(8,128)(2,1)S(1)}, u32[]{:S(2)}, u32[]{:S(2)}) collective-permute-start(bf16[512,1024]{1,0:T(8,128)(2,1)} %collective-permute-done.11), channel_id=1, source_target_pairs={{0,8},{8,0},{16,24},{24,16},{1,9},{9,1},{17,25},{25,17},{2,10},{10... | collective-permute-start | bytes 3145736 | tf_op jit(solution)/shard_map/ppermute | solution.py:509
  113.7 42.0 %collective-permute-start.15 = (bf16[512,1024]{1,0:T(8,128)(2,1)S(1)}, bf16[512,1024]{1,0:T(8,128)(2,1)S(1)}, u32[]{:S(2)}, u32[]{:S(2)}) collective-permute-start(bf16[512,1024]{1,0:T(8,128)(2,1)S(1)} %copy-done.78), channel_id=1, source_target_pairs={{0,1},{1,0},{2,3},{3,2},{4,5},{5,4},{6,7},{7,6},{8,9},{9,8},{10,11... | collective-permute-start | bytes 3145736 | tf_op jit(solution)/shard_map/ppermute | solution.py:480
  114.0 37.8 %collective-permute-start.14 = (bf16[512,1024]{1,0:T(8,128)(2,1)S(1)}, bf16[512,1024]{1,0:T(8,128)(2,1)S(1)}, u32[]{:S(2)}, u32[]{:S(2)}) collective-permute-start(bf16[512,1024]{1,0:T(8,128)(2,1)S(1)} %collective-permute-done.13), channel_id=1, source_target_pairs={{0,8},{8,0},{16,24},{24,16},{1,9},{9,1},{17,25},{25,17},{2,10},{10... | collective-permute-start | bytes 3145736 | tf_op jit(solution)/shard_map/ppermute | solution.py:509
  160.3 32.6 %collective-permute-start.19 = (bf16[512,1024]{1,0:T(8,128)(2,1)S(1)}, bf16[512,1024]{1,0:T(8,128)(2,1)S(1)}, u32[]{:S(2)}, u32[]{:S(2)}) collective-permute-start(bf16[512,1024]{1,0:T(8,128)(2,1)S(1)} %copy-done.77), channel_id=1, source_target_pairs={{0,1},{1,0},{2,3},{3,2},{4,5},{5,4},{6,7},{7,6},{8,9},{9,8},{10,11... | collective-permute-start | bytes 3145736 | tf_op jit(solution)/shard_map/ppermute | solution.py:480
  164.2 40.0 %collective-permute-start.32 = (bf16[2,128,2048]{2,1,0:T(8,128)(2,1)S(1)}, bf16[2,128,2048]{2,1,0:T(8,128)(2,1)S(1)}, u32[]{:S(2)}, u32[]{:S(2)}) collective-permute-start(bf16[2,128,2048]{2,1,0:T(8,128)(2,1)S(1)} %maximum_maximum_fusion.6), channel_id=1, source_target_pairs={{0,4},{2,6},{4,0},{6,2},{1,5},{3,7},{5,1},{7,3},{8,12},{10,14},{12... | collective-permute-start | bytes 3145736 | tf_op jit(solution)/shard_map/ppermute | solution.py:480
  192.9 25.6 %collective-permute-start.20 = (bf16[512,1024]{1,0:T(8,128)(2,1)S(1)}, bf16[512,1024]{1,0:T(8,128)(2,1)S(1)}, u32[]{:S(2)}, u32[]{:S(2)}) collective-permute-start(bf16[512,1024]{1,0:T(8,128)(2,1)S(1)} %constant_dynamic-slice_fusion), channel_id=1, source_target_pairs={{0,1},{1,0},{2,3},{3,2},{4,5},{5,4},{6,7},{7,6},{8,9},{9,8},{10,11... | collective-permute-start | bytes 3145736 | tf_op jit(solution)/shard_map/ppermute | solution.py:480
  204.1 26.0 %collective-permute-start.25 = (bf16[512,1024]{1,0:T(8,128)(2,1)S(1)}, bf16[512,1024]{1,0:T(8,128)(2,1)S(1)}, u32[]{:S(2)}, u32[]{:S(2)}) collective-permute-start(bf16[512,1024]{1,0:T(8,128)(2,1)S(1)} %collective-permute-done.19), channel_id=1, source_target_pairs={{0,8},{8,0},{16,24},{24,16},{1,9},{9,1},{17,25},{25,17},{2,10},{10... | collective-permute-start | bytes 3145736 | tf_op jit(solution)/shard_map/ppermute | solution.py:509
  204.4 47.8 %collective-permute-start.33 = (bf16[2,256,2048]{2,1,0:T(8,128)(2,1)S(1)}, bf16[2,256,2048]{2,1,0:T(8,128)(2,1)S(1)}, u32[]{:S(2)}, u32[]{:S(2)}) collective-permute-start(bf16[2,256,2048]{2,1,0:T(8,128)(2,1)S(1)} %pad_maximum_fusion.10), channel_id=1, source_target_pairs={{0,2},{2,0},{4,6},{6,4},{1,3},{3,1},{5,7},{7,5},{8,10},{10,8},{12,... | collective-permute-start | bytes 6291464 | tf_op jit(solution)/shard_map/ppermute | solution.py:480
  218.5 33.6 %collective-permute-start.34 = (bf16[512,1024]{1,0:T(8,128)(2,1)S(1)}, bf16[512,1024]{1,0:T(8,128)(2,1)S(1)}, u32[]{:S(2)}, u32[]{:S(2)}) collective-permute-start(bf16[512,1024]{1,0:T(8,128)(2,1)S(1)} %collective-permute-done.20), channel_id=1, source_target_pairs={{0,8},{8,0},{16,24},{24,16},{1,9},{9,1},{17,25},{25,17},{2,10},{10... | collective-permute-start | bytes 3145736 | tf_op jit(solution)/shard_map/ppermute | solution.py:509
  256.4 35.0 %collective-permute-start.26 = (bf16[128,2048]{1,0:T(8,128)(2,1)S(1)}, bf16[128,2048]{1,0:T(8,128)(2,1)S(1)}, u32[]{:S(2)}, u32[]{:S(2)}) collective-permute-start(bf16[128,2048]{1,0:T(8,128)(2,1)S(1)} %get-tuple-element.284), channel_id=1, source_target_pairs={{0,4},{2,6},{4,0},{6,2},{1,5},{3,7},{5,1},{7,3},{8,12},{10,14},{12... | collective-permute-start | bytes 1572872 | tf_op jit(solution)/shard_map/ppermute | solution.py:480
  295.9 26.5 %collective-permute-start.40 = (bf16[128,2048]{1,0:T(8,128)(2,1)S(1)}, bf16[128,2048]{1,0:T(8,128)(2,1)S(1)}, u32[]{:S(2)}, u32[]{:S(2)}) collective-permute-start(bf16[128,2048]{1,0:T(8,128)(2,1)S(1)} %split.186), channel_id=1, source_target_pairs={{0,4},{2,6},{4,0},{6,2},{1,5},{3,7},{5,1},{7,3},{8,12},{10,14},{12... | collective-permute-start | bytes 1572872 | tf_op jit(solution)/shard_map/ppermute | solution.py:480
  321.5 25.2 %collective-permute-start.41 = (bf16[512,1024]{1,0:T(8,128)(2,1)S(1)}, bf16[512,1024]{1,0:T(8,128)(2,1)S(1)}, u32[]{:S(2)}, u32[]{:S(2)}) collective-permute-start(bf16[512,1024]{1,0:T(8,128)(2,1)S(1)} %fusion.35), channel_id=1, source_target_pairs={{0,1},{1,0},{2,3},{3,2},{4,5},{5,4},{6,7},{7,6},{8,9},{9,8},{10,11... | collective-permute-start | bytes 3145736 | tf_op jit(solution)/shard_map/ppermute | solution.py:480
  356.3 33.9 %collective-permute-start.50 = (bf16[128,2048]{1,0:T(8,128)(2,1)S(1)}, bf16[128,2048]{1,0:T(8,128)(2,1)S(1)}, u32[]{:S(2)}, u32[]{:S(2)}) collective-permute-start(bf16[128,2048]{1,0:T(8,128)(2,1)S(1)} %get-tuple-element.272), channel_id=1, source_target_pairs={{0,4},{2,6},{4,0},{6,2},{1,5},{3,7},{5,1},{7,3},{8,12},{10,14},{12... | collective-permute-start | bytes 1572872 | tf_op jit(solution)/shard_map/ppermute | solution.py:480
  374.0 28.1 %collective-permute-start.53 = (bf16[512,1024]{1,0:T(8,128)(2,1)S(1)}, bf16[512,1024]{1,0:T(8,128)(2,1)S(1)}, u32[]{:S(2)}, u32[]{:S(2)}) collective-permute-start(bf16[512,1024]{1,0:T(8,128)(2,1)S(1)} %add_convert_fusion.36), channel_id=1, source_target_pairs={{8,16},{16,8},{9,17},{17,9},{10,18},{18,10},{11,19},{19,11},{12,20... | collective-permute-start | bytes 3145736 | tf_op jit(solution)/shard_map/ppermute | solution.py:877
  374.8 27.2 %collective-permute-start.52 = (bf16[512,1024]{1,0:T(8,128)(2,1)S(1)}, bf16[512,1024]{1,0:T(8,128)(2,1)S(1)}, u32[]{:S(2)}, u32[]{:S(2)}) collective-permute-start(bf16[512,1024]{1,0:T(8,128)(2,1)S(1)} %convolution_convert_fusion.13), channel_id=1, source_target_pairs={{0,1},{1,0},{2,3},{3,2},{4,5},{5,4},{6,7},{7,6},{8,9},{9,8},{10,11... | collective-permute-start | bytes 3145736 | tf_op jit(solution)/shard_map/ppermute | solution.py:480
  375.7 25.9 %collective-permute-start.54 = (bf16[512,1024]{1,0:T(8,128)(2,1)S(1)}, bf16[512,1024]{1,0:T(8,128)(2,1)S(1)}, u32[]{:S(2)}, u32[]{:S(2)}) collective-permute-start(bf16[512,1024]{1,0:T(8,128)(2,1)S(1)} %add_convert_fusion.35), channel_id=1, source_target_pairs={{0,8},{24,16},{1,9},{25,17},{2,10},{26,18},{3,11},{27,19},{4,12},{... | collective-permute-start | bytes 3145736 | tf_op jit(solution)/shard_map/ppermute | solution.py:890
  402.1 36.5 %collective-permute-start.56 = (bf16[512,1024]{1,0:T(8,128)(2,1)S(1)}, bf16[512,1024]{1,0:T(8,128)(2,1)S(1)}, u32[]{:S(2)}, u32[]{:S(2)}) collective-permute-start(bf16[512,1024]{1,0:T(8,128)(2,1)S(1)} %add_convert_fusion.34), channel_id=1, source_target_pairs={{8,16},{16,8},{9,17},{17,9},{10,18},{18,10},{11,19},{19,11},{12,20... | collective-permute-start | bytes 3145736 | tf_op jit(solution)/shard_map/ppermute | solution.py:877
  403.0 35.6 %collective-permute-start.55 = (bf16[512,1024]{1,0:T(8,128)(2,1)S(1)}, bf16[512,1024]{1,0:T(8,128)(2,1)S(1)}, u32[]{:S(2)}, u32[]{:S(2)}) collective-permute-start(bf16[512,1024]{1,0:T(8,128)(2,1)S(1)} %convolution_convert_fusion.12), channel_id=1, source_target_pairs={{0,1},{1,0},{2,3},{3,2},{4,5},{5,4},{6,7},{7,6},{8,9},{9,8},{10,11... | collective-permute-start | bytes 3145736 | tf_op jit(solution)/shard_map/ppermute | solution.py:480
  411.3 25.8 %collective-permute-start.57 = (bf16[512,1024]{1,0:T(8,128)(2,1)S(1)}, bf16[512,1024]{1,0:T(8,128)(2,1)S(1)}, u32[]{:S(2)}, u32[]{:S(2)}) collective-permute-start(bf16[512,1024]{1,0:T(8,128)(2,1)S(1)} %get-tuple-element.180), channel_id=1, source_target_pairs={{0,8},{8,0},{16,24},{24,16},{1,9},{9,1},{17,25},{25,17},{2,10},{10... | collective-permute-start | bytes 3145736 | tf_op jit(solution)/shard_map/ppermute | solution.py:890
  420.9 25.3 %collective-permute-start.36 = (bf16[2,128,2048]{2,1,0:T(8,128)(2,1)S(1)}, bf16[2,128,2048]{2,1,0:T(8,128)(2,1)S(1)}, u32[]{:S(2)}, u32[]{:S(2)}) collective-permute-start(bf16[2,128,2048]{2,1,0:T(8,128)(2,1)S(1)} %split.183), channel_id=1, source_target_pairs={{0,4},{2,6},{4,0},{6,2},{1,5},{3,7},{5,1},{7,3},{8,12},{10,14},{12... | collective-permute-start | bytes 3145736 | tf_op jit(solution)/shard_map/ppermute | solution.py:480
  438.6 65.7 %collective-permute-start.59 = (bf16[512,1024]{1,0:T(8,128)(2,1)}, bf16[512,1024]{1,0:T(8,128)(2,1)}, u32[]{:S(2)}, u32[]{:S(2)}) collective-permute-start(bf16[512,1024]{1,0:T(8,128)(2,1)} %add_convert_fusion.31), channel_id=1, source_target_pairs={{8,16},{16,8},{9,17},{17,9},{10,18},{18,10},{11,19},{19,11},{12,20... | collective-permute-start | bytes 3145736 | tf_op jit(solution)/shard_map/ppermute | solution.py:877
  451.2 32.5 %collective-permute-start.46 = (bf16[2,64,1024]{2,1,0:T(8,128)(2,1)S(1)}, bf16[2,64,1024]{2,1,0:T(8,128)(2,1)S(1)}, u32[]{:S(2)}, u32[]{:S(2)}) collective-permute-start(bf16[2,64,1024]{2,1,0:T(8,128)(2,1)S(1)} %get-tuple-element.353), channel_id=1, source_target_pairs={{16,0},{24,1},{20,2},{28,3},{17,4},{25,5},{21,6},{29,7},{18,8},{26... | collective-permute-start | bytes 786440 | tf_op jit(solution)/shard_map/ppermute | solution.py:679
  454.8 29.6 %collective-permute-start.47 = (bf16[2,64,1024]{2,1,0:T(8,128)(2,1)S(1)}, bf16[2,64,1024]{2,1,0:T(8,128)(2,1)}, u32[]{:S(2)}, u32[]{:S(2)}) collective-permute-start(bf16[2,64,1024]{2,1,0:T(8,128)(2,1)S(1)} %get-tuple-element.352), channel_id=1, source_target_pairs={{24,0},{16,1},{28,2},{20,3},{25,4},{17,5},{29,6},{21,7},{26,8},{18... | collective-permute-start | bytes 786440 | tf_op jit(solution)/shard_map/ppermute | solution.py:679
  466.0 36.6 %collective-permute-start.60 = (bf16[512,1024]{1,0:T(8,128)(2,1)}, bf16[512,1024]{1,0:T(8,128)(2,1)}, u32[]{:S(2)}, u32[]{:S(2)}) collective-permute-start(bf16[512,1024]{1,0:T(8,128)(2,1)} %get-tuple-element.184), channel_id=1, source_target_pairs={{0,8},{8,0},{16,24},{24,16},{1,9},{9,1},{17,25},{25,17},{2,10},{10... | collective-permute-start | bytes 3145736 | tf_op jit(solution)/shard_map/ppermute | solution.py:890
  490.0 27.2 %collective-permute-start.58 = (bf16[512,1024]{1,0:T(8,128)(2,1)S(1)}, bf16[512,1024]{1,0:T(8,128)(2,1)S(1)}, u32[]{:S(2)}, u32[]{:S(2)}) collective-permute-start(bf16[512,1024]{1,0:T(8,128)(2,1)S(1)} %fusion.41), channel_id=1, source_target_pairs={{0,1},{1,0},{2,3},{3,2},{4,5},{5,4},{6,7},{7,6},{8,9},{9,8},{10,11... | collective-permute-start | bytes 3145736 | tf_op jit(solution)/shard_map/ppermute | solution.py:480
  520.2 26.0 %collective-permute-start.63 = (bf16[512,1024]{1,0:T(8,128)(2,1)S(1)}, bf16[512,1024]{1,0:T(8,128)(2,1)S(1)}, u32[]{:S(2)}, u32[]{:S(2)}) collective-permute-start(bf16[512,1024]{1,0:T(8,128)(2,1)S(1)} %get-tuple-element.189), channel_id=1, source_target_pairs={{0,8},{8,0},{16,24},{24,16},{1,9},{9,1},{17,25},{25,17},{2,10},{10... | collective-permute-start | bytes 3145736 | tf_op jit(solution)/shard_map/ppermute | solution.py:890
  521.6 26.3 %collective-permute-start.61 = (bf16[512,1024]{1,0:T(8,128)(2,1)S(1)}, bf16[512,1024]{1,0:T(8,128)(2,1)S(1)}, u32[]{:S(2)}, u32[]{:S(2)}) collective-permute-start(bf16[512,1024]{1,0:T(8,128)(2,1)S(1)} %fusion.44), channel_id=1, source_target_pairs={{0,1},{1,0},{2,3},{3,2},{4,5},{5,4},{6,7},{7,6},{8,9},{9,8},{10,11... | collective-permute-start | bytes 3145736 | tf_op jit(solution)/shard_map/ppermute | solution.py:480
  547.9 32.2 %collective-permute-start.65 = (bf16[512,1024]{1,0:T(8,128)(2,1)S(1)}, bf16[512,1024]{1,0:T(8,128)(2,1)S(1)}, u32[]{:S(2)}, u32[]{:S(2)}) collective-permute-start(bf16[512,1024]{1,0:T(8,128)(2,1)S(1)} %add_convert_fusion.25), channel_id=1, source_target_pairs={{8,16},{16,8},{9,17},{17,9},{10,18},{18,10},{11,19},{19,11},{12,20... | collective-permute-start | bytes 3145736 | tf_op jit(solution)/shard_map/ppermute | solution.py:877
  550.1 29.3 %collective-permute-start.66 = (bf16[512,1024]{1,0:T(8,128)(2,1)S(1)}, bf16[512,1024]{1,0:T(8,128)(2,1)S(1)}, u32[]{:S(2)}, u32[]{:S(2)}) collective-permute-start(bf16[512,1024]{1,0:T(8,128)(2,1)S(1)} %get-tuple-element.194), channel_id=1, source_target_pairs={{0,8},{8,0},{16,24},{24,16},{1,9},{9,1},{17,25},{25,17},{2,10},{10... | collective-permute-start | bytes 3145736 | tf_op jit(solution)/shard_map/ppermute | solution.py:890
  592.6 48.8 %collective-permute-start.69 = (bf16[512,1024]{1,0:T(8,128)(2,1)S(1)}, bf16[512,1024]{1,0:T(8,128)(2,1)S(1)}, u32[]{:S(2)}, u32[]{:S(2)}) collective-permute-start(bf16[512,1024]{1,0:T(8,128)(2,1)S(1)} %get-tuple-element.198), channel_id=1, source_target_pairs={{0,8},{8,0},{16,24},{24,16},{1,9},{9,1},{17,25},{25,17},{2,10},{10... | collective-permute-start | bytes 3145736 | tf_op jit(solution)/shard_map/ppermute | solution.py:890
  649.6 25.3 %collective-permute-start.72 = (bf16[512,1024]{1,0:T(8,128)(2,1)S(1)}, bf16[512,1024]{1,0:T(8,128)(2,1)S(1)}, u32[]{:S(2)}, u32[]{:S(2)}) collective-permute-start(bf16[512,1024]{1,0:T(8,128)(2,1)S(1)} %get-tuple-element.202), channel_id=1, source_target_pairs={{0,8},{8,0},{16,24},{24,16},{1,9},{9,1},{17,25},{25,17},{2,10},{10... | collective-permute-start | bytes 3145736 | tf_op jit(solution)/shard_map/ppermute | solution.py:890
  739.0 45.7 %collective-permute-start.92 = (bf16[512,1024]{1,0:T(8,128)(2,1)}, bf16[512,1024]{1,0:T(8,128)(2,1)S(1)}, u32[]{:S(2)}, u32[]{:S(2)}) collective-permute-start(bf16[512,1024]{1,0:T(8,128)(2,1)} %get-tuple-element.213), channel_id=1, source_target_pairs={{0,8},{8,0},{16,24},{24,16},{1,9},{9,1},{17,25},{25,17},{2,10},{10... | collective-permute-start | bytes 3145736 | tf_op jit(solution)/shard_map/ppermute | solution.py:890
  785.3 25.6 %collective-permute-start.96 = (bf16[512,1024]{1,0:T(8,128)(2,1)S(1)}, bf16[512,1024]{1,0:T(8,128)(2,1)S(1)}, u32[]{:S(2)}, u32[]{:S(2)}) collective-permute-start(bf16[512,1024]{1,0:T(8,128)(2,1)S(1)} %copy-done.183), channel_id=1, source_target_pairs={{0,8},{8,0},{16,24},{24,16},{1,9},{9,1},{17,25},{25,17},{2,10},{10... | collective-permute-start | bytes 3145736 | tf_op jit(solution)/shard_map/ppermute | solution.py:890
  786.2 25.3 %collective-permute-start.95 = (bf16[512,1024]{1,0:T(8,128)(2,1)S(1)}, bf16[512,1024]{1,0:T(8,128)(2,1)S(1)}, u32[]{:S(2)}, u32[]{:S(2)}) collective-permute-start(bf16[512,1024]{1,0:T(8,128)(2,1)S(1)} %add_convert_fusion.8), channel_id=1, source_target_pairs={{8,16},{16,8},{9,17},{17,9},{10,18},{18,10},{11,19},{19,11},{12,20... | collective-permute-start | bytes 3145736 | tf_op jit(solution)/shard_map/ppermute | solution.py:877
  788.0 31.4 %collective-permute-start.82 = (bf16[128,2048]{1,0:T(8,128)(2,1)S(1)}, bf16[128,2048]{1,0:T(8,128)(2,1)S(1)}, u32[]{:S(2)}, u32[]{:S(2)}) collective-permute-start(bf16[128,2048]{1,0:T(8,128)(2,1)S(1)} %split.184), channel_id=1, source_target_pairs={{0,4},{2,6},{4,0},{6,2},{1,5},{3,7},{5,1},{7,3},{8,12},{10,14},{12... | collective-permute-start | bytes 1572872 | tf_op jit(solution)/shard_map/ppermute | solution.py:480
  788.5 28.6 %collective-permute-start.74 = (bf16[128,2048]{1,0:T(8,128)(2,1)S(1)}, bf16[128,2048]{1,0:T(8,128)(2,1)S(1)}, u32[]{:S(2)}, u32[]{:S(2)}) collective-permute-start(bf16[128,2048]{1,0:T(8,128)(2,1)S(1)} %split.185), channel_id=1, source_target_pairs={{0,4},{2,6},{4,0},{6,2},{1,5},{3,7},{5,1},{7,3},{8,12},{10,14},{12... | collective-permute-start | bytes 1572872 | tf_op jit(solution)/shard_map/ppermute | solution.py:480
  811.4 40.3 %collective-permute-start.98 = (bf16[512,1024]{1,0:T(8,128)(2,1)S(1)}, bf16[512,1024]{1,0:T(8,128)(2,1)S(1)}, u32[]{:S(2)}, u32[]{:S(2)}) collective-permute-start(bf16[512,1024]{1,0:T(8,128)(2,1)S(1)} %add_convert_fusion.3), channel_id=1, source_target_pairs={{8,16},{16,8},{9,17},{17,9},{10,18},{18,10},{11,19},{19,11},{12,20... | collective-permute-start | bytes 3145736 | tf_op jit(solution)/shard_map/ppermute | solution.py:877
  812.7 41.9 %collective-permute-start.97 = (bf16[512,1024]{1,0:T(8,128)(2,1)S(1)}, bf16[512,1024]{1,0:T(8,128)(2,1)S(1)}, u32[]{:S(2)}, u32[]{:S(2)}) collective-permute-start(bf16[512,1024]{1,0:T(8,128)(2,1)S(1)} %add_convert_fusion.6), channel_id=1, source_target_pairs={{8,0},{16,24},{9,1},{17,25},{10,2},{18,26},{11,3},{19,27},{12,4},{... | collective-permute-start | bytes 3145736 | tf_op jit(solution)/shard_map/ppermute | solution.py:890
  848.2 31.5 %collective-permute-start.83 = (bf16[2,64,1024]{2,1,0:T(8,128)(2,1)S(1)}, bf16[2,64,1024]{2,1,0:T(8,128)(2,1)S(1)}, u32[]{:S(2)}, u32[]{:S(2)}) collective-permute-start(bf16[2,64,1024]{2,1,0:T(8,128)(2,1)S(1)} %get-tuple-element.351), channel_id=1, source_target_pairs={{0,0},{8,1},{4,2},{12,3},{1,4},{9,5},{5,6},{13,7},{2,8},{10,9},{6,... | collective-permute-start | bytes 786440 | tf_op jit(solution)/shard_map/ppermute | solution.py:679
  848.9 30.8 %collective-permute-start.84 = (bf16[2,64,1024]{2,1,0:T(8,128)(2,1)S(1)}, bf16[2,64,1024]{2,1,0:T(8,128)(2,1)S(1)}, u32[]{:S(2)}, u32[]{:S(2)}) collective-permute-start(bf16[2,64,1024]{2,1,0:T(8,128)(2,1)S(1)} %get-tuple-element.350), channel_id=1, source_target_pairs={{8,0},{0,1},{12,2},{4,3},{9,4},{1,5},{13,6},{5,7},{10,8},{2,9},{14... | collective-permute-start | bytes 786440 | tf_op jit(solution)/shard_map/ppermute | solution.py:679
  851.7 28.1 %collective-permute-start.85 = (bf16[2,64,1024]{2,1,0:T(8,128)(2,1)S(1)}, bf16[2,64,1024]{2,1,0:T(8,128)(2,1)S(1)}, u32[]{:S(2)}, u32[]{:S(2)}) collective-permute-start(bf16[2,64,1024]{2,1,0:T(8,128)(2,1)S(1)} %get-tuple-element.349), channel_id=1, source_target_pairs={{16,0},{24,1},{20,2},{28,3},{17,4},{25,5},{21,6},{29,7},{18,8},{26... | collective-permute-start | bytes 786440 | tf_op jit(solution)/shard_map/ppermute | solution.py:679
  851.7 25.5 %collective-permute-start.91 = (f32[4,1024]{1,0:T(4,128)S(1)}, f32[4,1024]{1,0:T(4,128)S(1)}, u32[]{:S(2)}, u32[]{:S(2)}) collective-permute-start(f32[4,1024]{1,0:T(4,128)S(1)} %slice_add_fusion.7), channel_id=1, source_target_pairs={{0,4},{2,6},{4,0},{6,2},{1,5},{3,7},{5,1},{7,3},{8,12},{10,14},{12... | collective-permute-start | bytes 49160 | tf_op jit(solution)/shard_map/ppermute | solution.py:480
  854.6 26.5 %collective-permute-start.86 = (bf16[2,64,1024]{2,1,0:T(8,128)(2,1)S(1)}, bf16[2,64,1024]{2,1,0:T(8,128)(2,1)}, u32[]{:S(2)}, u32[]{:S(2)}) collective-permute-start(bf16[2,64,1024]{2,1,0:T(8,128)(2,1)S(1)} %get-tuple-element.263), channel_id=1, source_target_pairs={{24,0},{16,1},{28,2},{20,3},{25,4},{17,5},{29,6},{21,7},{26,8},{18... | collective-permute-start | bytes 786440 | tf_op jit(solution)/shard_map/ppermute | solution.py:679
  (247 other events, 4153.1 us)
